TPU v7x, 256 devices: a whole 4x4x8 slice. The times are simulated.
256 devices in a mesh: frames: 4 (over z_hi), states: 64 (over z_lo, y, x, core).
Axes of the slice: x: 4, y: 4, z: 8 (z_hi: 4, z_lo: 2; z = z_hi * 2 + z_lo), core: 2. Of those that a mesh axis runs over, the one named last changes fastest.
Arguments:
- features: bfloat16 [16384, 1024], P('states', 'frames'), may hold values from -10 to 10
- state_ids: int32 [16384, 32], P('states'), may hold values from 0 to 6143, as said below
- weights: float32 [16384, 32], P('states'), may hold values from 0.05 to 1
Outputs:
- means: bfloat16 [6144, 1024], P(None, 'frames')
- precisions: bfloat16 [6144, 1024], P(None, 'frames')
- frame_score: float32 [16384], P('states')
Inputs may be any that keep to these rules, and one draw needn't show every extreme that they name: `state_ids`: each row names 32 different states; every state is named by some row.
All inputs are finite; a program needn't handle non-finite values.
Results may differ from a plain program's by a relative error of at most 0.0034.
Values may be sent and summed in bfloat16 or wider, within the bound.
A program may use at most 128 MiB of HBM per device.

v0:
```python
import jax
import jax.numpy as jnp
from jax import lax
from jax.sharding import PartitionSpec as P

D = 1024
STATE_DEV = 96


variance_floor = 0.25


def copy_for_each(shard, axis):
    copies = jnp.broadcast_to(shard, (lax.axis_size(axis), *shard.shape))
    return lax.all_to_all(copies, axis, split_axis=0, concat_axis=0, tiled=True)


def taken_together(shard, axis):
    everything = copy_for_each(shard, axis)
    return jnp.sum(everything, axis=0)


def refresh(first, second, counts):
    mean_value = first / counts
    variance = jnp.maximum(second / counts - mean_value * mean_value, variance_floor)
    return (mean_value.astype(jnp.bfloat16), (1.0 / variance).astype(jnp.bfloat16))


def per_device(features, state_ids, weights):
    rows_here, local_width = features.shape
    group_size = lax.axis_size("states")
    total_states = STATE_DEV * group_size
    row_index = jnp.arange(rows_here, dtype=jnp.int32)[:, None]
    rounded = weights.astype(jnp.bfloat16)
    posterior = (
        jnp.zeros((rows_here, total_states), jnp.bfloat16).at[row_index, state_ids].add(rounded)
    )
    values = features.astype(jnp.float32)
    squares = (values * values).astype(jnp.bfloat16)
    blocked = posterior.reshape(rows_here, group_size, STATE_DEV)
    routed = lax.all_to_all(blocked, "states", split_axis=1, concat_axis=0, tiled=True)
    routed = routed.reshape(rows_here * group_size, STATE_DEV)
    owned_counts = jnp.sum(routed, axis=0, dtype=jnp.float32)
    piece = lax.all_gather(features, "states", axis=0, tiled=True)
    piece_f = piece.astype(jnp.float32)
    piece_sq = (piece_f * piece_f).astype(jnp.bfloat16)
    joined = jnp.concatenate([piece, piece_sq], axis=1)
    owned_sums = lax.dot_general(
        routed, joined, (((0,), (0,)), ((), ())), preferred_element_type=jnp.float32
    )
    mean_rows, prec_rows = refresh(
        owned_sums[:, :local_width], owned_sums[:, local_width:], owned_counts[:, None]
    )
    packed = lax.all_gather(
        jnp.concatenate([mean_rows, prec_rows], axis=1), "states", axis=0, tiled=True
    )
    means = packed[:, :local_width]
    precisions = packed[:, local_width:]
    mean_f = means.astype(jnp.float32)
    prec_f = precisions.astype(jnp.float32)
    product = (mean_f * prec_f).astype(jnp.bfloat16)
    constant_term = jnp.sum(mean_f * product.astype(jnp.float32) - jnp.log(prec_f), axis=1)
    lookup_table = jnp.concatenate([precisions, product], axis=1)
    weight_f = rounded.astype(jnp.float32)
    blended = jnp.dot(posterior, lookup_table, preferred_element_type=jnp.float32)
    quadratic = jnp.sum(
        squares.astype(jnp.float32) * blended[:, :local_width]
        - 2.0 * values * blended[:, local_width:],
        axis=1,
    )
    quadratic = quadratic + jnp.sum(weight_f * constant_term[state_ids], axis=1)
    summed = taken_together(quadratic, "frames")
    weight_sum = jnp.sum(weight_f, axis=1)
    frame_score = -0.5 * summed / (D * weight_sum)
    return (means, precisions, frame_score)


def solution(mesh):
    return jax.shard_map(
        per_device,
        mesh=mesh,
        in_specs=(P("states", "frames"), P("states", None), P("states", None)),
        out_specs=(P(None, "frames"), P(None, "frames"), P("states")),
        check_vma=False,
    )
```

profile of v0, /device:TPU:1, one launch (start us, length us, event | category | flops | bytes accessed | tf_op | source)
XLA Modules:
  0.0 357.3 jit_solution(10742842729083389817)
XLA Ops:
  7.2 0.7 all-gather.3.cloned.1.call-update
  7.9 0.9 copy.20
  8.8 0.1 reshape.37
  8.9 0.8 compare_select_fusion
  9.7 0.7 multiply_reduce_fusion
  10.4 0.7 and_reduce_fusion
  11.2 0.1 copy.19
  11.3 0.1 reshape.35
  11.4 57.8 %scatter_custom_fusion = bf16[1572864]{0:T(1024)(128)(2,1)S(1)} fusion(s32[8192]{0:T(1024)S(1)} %reshape.35, bf16[8192]{0:T(1024)(128)(2,1)S(1)} %reshape.37, bf16[]{:T(256)} %constant.9.clone.1), kind=kCustom, calls=%fused_computation.18 | custom fusion | flops 8192 | bytes 3145730
  69.2 4.0 %reshape.20 = bf16[256,64,96]{2,1,0:T(8,128)(2,1)} reshape(bf16[1572864]{0:T(1024)(128)(2,1)S(1)} %scatter_custom_fusion) | data formatting | bytes 6291456 | tf_op jit(solution)/shard_map/reshape | solution.py:40
  73.2 6.5 %copy.21 = bf16[256,64,96]{0,2,1:T(8,128)(2,1)} copy(bf16[256,64,96]{2,1,0:T(8,128)(2,1)} %reshape.20) | data formatting | bytes 6291456 | tf_op jit(solution)/shard_map/reshape | solution.py:40
  79.8 53.7 %all_to_all.21 = bf16[256,64,96]{0,2,1:T(8,128)(2,1)S(1)} all-to-all(bf16[256,64,96]{0,2,1:T(8,128)(2,1)} %copy.21), channel_id=1, replica_groups=mesh['frames'=4,'states'=64] {'states'}, dimensions={1} | all-to-all | bytes 6291456 | tf_op jit(solution)/shard_map/all_to_all | solution.py:41
  133.5 1.9 copy.26
  135.4 0.5 convert_reduce_fusion
  136.0 18.4 %all-gather.3.cloned.1.call-done = bf16[16384,256]{1,0:T(8,128)(2,1)} async-done(((bf16[256,256]{1,0:T(8,128)(2,1)}), bf16[16384,256]{1,0:T(8,128)(2,1)}) %all-gather.3.cloned.1.call-update) | async-done | bytes 8388624 | tf_op jit(solution)/shard_map/all_gather | solution.py:44
  154.4 8.7 %multiply_convert_fusion = bf16[16384,256]{1,0:T(8,128)(2,1)} fusion(bf16[16384,256]{1,0:T(8,128)(2,1)} %all-gather.3.cloned.1.call-done), kind=kLoop, calls=%fused_computation.6 | loop fusion | flops 12582912 | bytes 16777216 | tf_op jit(solution)/shard_map/convert_element_type | solution.py:46
  163.1 1.1 copy-done.2
  164.2 8.5 %fusion = f32[96,512]{1,0:T(8,128)S(1)} fusion(bf16[16384,96]{0,1:T(8,128)(2,1)S(1)} %bitcast.16, bf16[16384,256]{1,0:T(8,128)(2,1)} %multiply_convert_fusion, bf16[16384,256]{1,0:T(8,128)(2,1)S(1)} %copy-done), kind=kOutput, calls=%fused_computation.2 | convolution fusion | flops 1644167168 | bytes 20119552 | tf_op jit(solution)/shard_map/dot_general | solution.py:48
  172.7 0.1 fusion.22
  172.9 0.6 pad_maximum_fusion
  173.5 2.9 reshape.25
  176.4 0.1 copy.23
  176.5 0.1 reshape.29
  176.6 108.2 %all-gather.5.cloned.1.call-done = bf16[6144,512]{1,0:T(8,128)(2,1)} async-done(((bf16[96,512]{1,0:T(8,128)(2,1)}), bf16[6144,512]{1,0:T(8,128)(2,1)}) %all-gather.5.cloned.1.call-update) | async-done | bytes 6291472 | tf_op jit(solution)/shard_map/all_gather | solution.py:54
  284.9 4.9 %fusion.5 = (f32[6144]{0:T(1024)S(1)}, bf16[6144,256]{1,0:T(8,128)(2,1)S(1)}, bf16[6144,256]{1,0:T(8,128)(2,1)S(1)}, bf16[6144,256]{1,0:T(8,128)(2,1)}) fusion(bf16[6144,512]{1,0:T(8,128)(2,1)} %all-gather.5.cloned.1.call-done), kind=kLoop, calls=%fused_computation.11 | loop fusion | flops 12576768 | bytes 15753216 | tf_op jit(solution)/shard_map/reduce_sum | solution.py:62
  289.7 1.8 fusion.7
  291.6 0.1 fusion.16
  291.7 45.5 %gather_fusion = f32[8192]{0:T(1024)S(1)} fusion(f32[6144]{0:T(1024)S(1)} %get-tuple-element.5, s32[8192]{0:T(1024)S(1)} %broadcast_clamp_fusion), kind=kCustom, calls=%fused_computation | custom fusion | bytes 98304 | tf_op jit(solution)/shard_map/gather | solution.py:71
  337.3 0.1 reshape.28
  337.4 0.2 fusion.17
  337.5 12.4 %all_to_all.22 = f32[4,1,256]{2,1,0:T(1,128)S(1)} all-to-all(f32[4,1,256]{2,1,0:T(1,128)S(1)} %broadcast_in_dim.20), channel_id=1, replica_groups=mesh['frames'=4,'states'=64] {'frames'}, dimensions={0} | all-to-all | bytes 8192 | tf_op jit(solution)/shard_map/all_to_all | solution.py:15
  349.9 0.6 multiply_divide_fusion
  (18 shorter events, 0.2 us)
Async XLA Ops:
  7.2 147.2 %all-gather.3.cloned.1.call-start = ((), (), s32[]{:S(2)}) async-start(), calls=%async_computation.2 | async-start | bytes 8519680 | tf_op jit(solution)/shard_map/all_gather | solution.py:44
  7.9 277.0 %all-gather.5.cloned.1.call-start = ((), (), s32[]{:S(2)}) async-start(), calls=%async_computation.3 | async-start | bytes 6389760 | tf_op jit(solution)/shard_map/all_gather | solution.py:54
  154.4 8.7 %copy-start = (bf16[16384,256]{1,0:T(8,128)(2,1)S(1)}, bf16[16384,256]{1,0:T(8,128)(2,1)}, u32[]{:S(2)}) copy-start(bf16[16384,256]{1,0:T(8,128)(2,1)} %all-gather.3.cloned.1.call-done) | copy-start | bytes 25165828
  154.4 9.8 %copy-start.2 = (bf16[12,8,64,256]{3,1,2,0:T(8,128)(2,1)S(1)}, bf16[12,8,64,256]{3,1,2,0:T(8,128)(2,1)}, u32[]{:S(2)}) copy-start(bf16[12,8,64,256]{3,1,2,0:T(8,128)(2,1)} %copy.26) | copy-start | bytes 9437188
  176.6 113.1 %copy-start.1 = (bf16[256,6144]{1,0:T(8,128)(2,1)S(1)}, bf16[256,6144]{1,0:T(8,128)(2,1)}, u32[]{:S(2)}) copy-start(bf16[256,6144]{1,0:T(8,128)(2,1)} %reshape.25) | copy-start | bytes 9437188
  289.7 1.9 copy-start.3
  289.7 1.9 copy-start.4
Sparse Core Ops, SparseCore 0:
  9.8 144.4 all-gather.2
  173.6 111.1 all-gather.4
where the time goes:
time: 358 us; the launch traced here: 357 us
  waiting for transfers between devices  127 us (35%)
  other arithmetic  75.8 us (21%)
  blocking collectives  66.1 us (18%)
  local copies, waits for them, and re-layouts  63.5 us (18%)
  between operations  14.2 us (4%)
  matrix products  10.4 us (3%)
    all_gather x1, waiting for transfers between devices, per_device(): lax.all_gather(jnp.concatenate([mean_rows, prec_rows], axis=1), 'states',...  108 us
    unnamed x4, other arithmetic  59.3 us
    all_to_all x1, blocking collectives, per_device(): lax.all_to_all(blocked, 'states', split_axis=1, concat_axis=0, tiled=True)  53.7 us
    gather x2, local copies, waits for them, and re-layouts, per_device(): quadratic = quadratic + jnp.sum(weight_f * constant_term[state_ids], axis=1)  45.6 us
    all_gather x1, waiting for transfers between devices, per_device(): piece = lax.all_gather(features, 'states', axis=0, tiled=True)  18.4 us
    all_to_all x1, blocking collectives, copy_for_each(): return lax.all_to_all(copies, axis, split_axis=0, concat_axis=0, tiled=True)  12.4 us
    reshape x2, local copies, waits for them, and re-layouts, per_device(): blocked = posterior.reshape(rows_here, group_size, STATE_DEV)  10.5 us
    convert_element_type x1, other arithmetic, per_device(): piece_sq = (piece_f * piece_f).astype(jnp.bfloat16)  8.71 us
  transfers between devices with their start and end apart: 2, of which 2 were waited for; matrix products, arithmetic and copies ran while one was open for 22% of the time, Pallas kernels for 0%

commit v1 on v0

v1 whole, which is shorter than its diff:
```python
import jax
import jax.numpy as jnp
from jax import lax
from jax.experimental import pallas as pl
from jax.experimental.pallas import tpu as pltpu
from jax.sharding import PartitionSpec as P

MESH = pl.DeviceIdType.MESH
F32, BF16, I16, I32 = jnp.float32, jnp.bfloat16, jnp.int16, jnp.int32
D = 1024
W = 256
ROWS = 96
OWN = 48
FLOOR = 0.25


def msg(k, j):
    return k * (k + 1) // 2 + j + 1


def flip(s, k):
    return s + 2**k * (1 - 2 * ((s // 2**k) % 2))


def sibling(s, j):
    if j < 0:
        return s, 1
    b = s // 2**j
    return (b + 1 - 2 * (b % 2)) * 2**j, 2**j


def rev4(s):
    return (s % 2) * 8 + ((s // 2) % 2) * 4 + ((s // 4) % 2) * 2 + s // 8


class Flood:
    def __init__(self, views, ssem, rsem, slot, slot_other, partners, core, c):
        self.views, self.ssem, self.rsem = views, ssem, rsem
        self.slot, self.slot_other, self.partners, self.core, self.c = slot, slot_other, partners, core, c

    def _copies(self, region, block, i, device):
        out = []
        for a, view in enumerate(self.views):
            ref = view(region, *block)
            out.append(
                pltpu.make_async_remote_copy(
                    src_ref=ref, dst_ref=ref, send_sem=self.ssem.at[i, a], recv_sem=self.rsem.at[i, a],
                    device_id={"states": device}, device_id_type=MESH,
                )
            )
        return out

    def _out(self, k, j):
        return self._copies(self.c, sibling(self.slot, j), msg(k, j), self.partners[k])

    def _in(self, k, j):
        return self._copies(self.c, sibling(flip(self.slot, k), j), msg(k, j), self.partners[k])

    def _core_out(self, k, j):
        s = self.slot if k < 0 else flip(self.slot, k)
        return self._copies(self.c, sibling(s, j), 10 if k < 0 else 11 + msg(k, j), self.core)

    def _core_in(self, k, j):
        s = self.slot_other if k < 0 else flip(self.slot_other, k)
        return self._copies(1 - self.c, sibling(s, j), 10 if k < 0 else 11 + msg(k, j), self.core)

    def start(self):
        for k in range(4):
            for cp in self._out(k, -1):
                cp.start()
        for cp in self._core_out(-1, -1):
            cp.start()

    def arrive(self, k):
        for j in range(-1, k):
            for cp in self._in(k, j):
                cp.wait_recv()
            for cp in self._core_out(k, j):
                cp.start()
        for later in range(k + 1, 4):
            for cp in self._out(later, k):
                cp.start()

    def arrive_core(self, k):
        for j in range(-1, k) if k >= 0 else (-1,):
            for cp in self._core_in(k, j):
                cp.wait_recv()

    def finish(self):
        for k in range(4):
            for j in range(-1, k):
                for cp in self._out(k, j):
                    cp.wait_send()
                for cp in self._core_out(k, j):
                    cp.wait_send()
        for cp in self._core_out(-1, -1):
            cp.wait_send()


def kernel(
    x_ref, ids_ref, w_ref, om_ref, op_ref, score_ref,
    xs, sq, g, post, acc, racc, qb, rq, q8, q4, q2, q1, r8, r4, r2, r1, rh,
    g_s, g_r, x_s, x_r, o_s, o_r, z_s, z_r, q_s, q_r, h_s, h_r,
):
    me = lax.axis_index("states")
    hi = lax.axis_index("frames")
    c = me % 2
    x = (me // 2) % 4
    y = (me // 8) % 4
    z = me // 32

    def device(z, y, x, c):
        return ((z * 4 + y) * 4 + x) * 2 + c

    p = x + c * (y - x)
    q = y + c * (x - y)

    def at(p2, q2):
        return device(z, q2 + c * (p2 - q2), p2 + c * (q2 - p2), c)

    v0, v1, v2, v3 = (p + p // 2) % 2, p // 2, (q + q // 2) % 2, q // 2
    near = [at(p + 1 - 2 * (p % 2), q), at(3 - p, q), at(p, q + 1 - 2 * (q % 2)), at(p, 3 - q)]
    core = device(z, y, x, 1 - c)
    up = device(1 - z, y, x, c)
    slot = (v0 + 2 * v1 + 4 * v2 + 8 * v3, v3 + 2 * v2 + 4 * v1 + 8 * v0)
    other = (v2 + 2 * v3 + 4 * v0 + 8 * v1, v1 + 2 * v0 + 4 * v3 + 8 * v2)

    barrier = pltpu.get_barrier_semaphore()
    for d in near + [core, up]:
        pl.semaphore_signal(barrier, inc=1, device_id={"states": d}, device_id_type=MESH)
    for d in range(1, 4):
        pl.semaphore_signal(barrier, inc=1, device_id={"frames": (hi + d) % 4}, device_id_type=MESH)

    codes = jnp.transpose(ids_ref[...])
    w_t = jnp.transpose(w_ref[...]).astype(BF16).astype(F32)
    g[c, slot[0], 0:32, :] = codes.astype(I16)
    g[c, slot[0], 32:64, :] = (w_t * 4096.0).astype(I32).astype(I16)
    for f in range(2):
        xs[f, c, pl.ds(pl.multiple_of(slot[f] * 128, 128), 128), :] = x_ref[f * 128 : (f + 1) * 128, :]
    acc[...] = jnp.zeros_like(acc)
    pl.semaphore_wait(barrier, 9)

    gf = Flood([lambda r, s, n: g.at[r, pl.ds(s, n)]], g_s, g_r, slot[0], other[0], near, core, c)

    def x_view(f):
        return lambda r, s, n: xs.at[f, r, pl.ds(pl.multiple_of(s * 128, 128), n * 128)]

    orders = (near, near[::-1])
    xf = [Flood([x_view(f)], x_s.at[f], x_r.at[f], slot[f], other[f], orders[f], core, c) for f in range(2)]
    gf.start()
    for f in range(2):
        xf[f].start()

    base = [pl.multiple_of(((c * 2 + part) * 16 + slot[part]) * ROWS, ROWS) for part in range(2)]
    iota = lax.broadcasted_iota(I32, (ROWS, 128), 0)
    rows = jnp.concatenate([(iota + base[0]).astype(I16), (iota + base[1]).astype(I16)], axis=0)

    def build_one(ch, s):
        ids = g[ch, s, 0:32, :].astype(I32)
        wv = g[ch, s, 32:64, :].astype(I32).astype(F32) * (1.0 / 4096.0)
        for f in range(2):
            lanes = slice(f * 128, (f + 1) * 128)
            block = jnp.zeros((2 * ROWS, 128), BF16)
            for j in range(32):
                idj = jnp.broadcast_to(ids[j : j + 1, lanes].astype(I16), (2 * ROWS, 128))
                wj = jnp.broadcast_to(wv[j : j + 1, lanes].astype(BF16), (2 * ROWS, 128))
                block = jnp.where(rows == idj, wj, block)
            col = pl.multiple_of((s if f == 0 else rev4(s)) * 128, 128)
            post[f, ch, :, pl.ds(col, 128)] = block
            acc[:, 512:640] += block.astype(F32)

    def build(ch, start, n):
        if n == 1:
            build_one(ch, start)
        else:
            @pl.loop(0, n)
            def _(i):
                build_one(ch, start + i)

    def moments(f, ch, start, n):
        r = pl.ds(pl.multiple_of(start * 128, 128), n * 128)
        xv = xs[f, ch, r, :]
        xw = xv.astype(F32)
        sv = (xw * xw).astype(BF16)
        sq[f, ch, r, :] = sv
        pv = post[f, ch, :, r]
        acc[:, 0:256] += jnp.dot(pv, xv, preferred_element_type=F32)
        acc[:, 256:512] += jnp.dot(pv, sv, preferred_element_type=F32)

    def x_step(k):
        for f in range(2):
            xf[f].arrive(k)

    def x_core(k):
        for f in range(2):
            xf[f].arrive_core(k)

    build(c, slot[0], 1)
    gf.arrive_core(-1)
    build(1 - c, other[0], 1)
    gf.arrive(0)
    build(c, *sibling(slot[0], 0))
    gf.arrive_core(0)
    build(1 - c, *sibling(other[0], 0))
    gf.arrive(1)
    x_step(0)
    build(c, *sibling(slot[0], 1))
    gf.arrive_core(1)
    build(1 - c, *sibling(other[0], 1))
    gf.arrive(2)
    x_step(1)
    build(c, *sibling(slot[0], 2))
    gf.arrive_core(2)
    build(1 - c, *sibling(other[0], 2))
    gf.arrive(3)
    x_step(2)
    build(c, *sibling(slot[0], 3))
    gf.arrive_core(3)
    build(1 - c, *sibling(other[0], 3))
    for k in range(-1, 3):
        x_core(k)
        for f in range(2):
            moments(f, c, *sibling(slot[f], k))
            moments(f, 1 - c, *sibling(other[f], k))
    x_step(3)
    for f in range(2):
        moments(f, c, *sibling(slot[f], 3))
    x_core(3)
    for f in range(2):
        moments(f, 1 - c, *sibling(other[f], 3))

    def acc_copy(part):
        return pltpu.make_async_remote_copy(
            src_ref=acc.at[pl.ds(pl.multiple_of(part * ROWS + (1 - z) * OWN, 8), OWN)], dst_ref=racc.at[part],
            send_sem=z_s.at[part], recv_sem=z_r.at[part], device_id={"states": up}, device_id_type=MESH,
        )

    def own_rows(part, zz):
        return pl.ds(pl.multiple_of(base[part] + zz * OWN, 16), OWN)

    def up_copies(part, zz):
        return [
            pltpu.make_async_remote_copy(
                src_ref=ref.at[own_rows(part, zz)], dst_ref=ref.at[own_rows(part, zz)],
                send_sem=z_s.at[2 + part * 2 + a], recv_sem=z_r.at[2 + part * 2 + a],
                device_id={"states": up}, device_id_type=MESH,
            )
            for a, ref in enumerate((om_ref, op_ref))
        ]

    for part in range(2):
        acc_copy(part).start()
    for part in range(2):
        acc_copy(part).wait_recv()
        total = acc[pl.ds(pl.multiple_of(part * ROWS + z * OWN, 8), OWN), :] + racc[part]
        inv_count = jnp.sum(total[:, 512:640], axis=1, keepdims=True)
        mean = total[:, 0:256] / inv_count
        var = jnp.maximum(total[:, 256:512] / inv_count - mean * mean, FLOOR)
        om_ref[own_rows(part, z), :] = mean.astype(BF16)
        op_ref[own_rows(part, z), :] = (1.0 / var).astype(BF16)
        for cp in up_copies(part, z):
            cp.start()

    def o_view(ref, part):
        def view(r, s, n):
            start = pl.multiple_of(((r * 2 + part) * 16 + s) * ROWS, ROWS)
            return ref.at[pl.ds(start, n * ROWS)]
        return view

    of = [
        Flood([o_view(om_ref, t), o_view(op_ref, t)], o_s.at[t], o_r.at[t], slot[t], other[t], orders[t], core, c)
        for t in range(2)
    ]
    for part in range(2):
        for cp in up_copies(part, 1 - z):
            cp.wait_recv()
        of[part].start()

    def o_step(k):
        for t in range(2):
            of[t].arrive(k)

    both = [pl.ds(base[part], ROWS) for part in range(2)]
    mean_b = jnp.concatenate([om_ref[r, :] for r in both], axis=0)
    prec_b = jnp.concatenate([op_ref[r, :] for r in both], axis=0)
    mean_f, prec_f = mean_b.astype(F32), prec_b.astype(F32)
    prod_f = (mean_f * prec_f).astype(BF16).astype(F32)
    minus2 = (-2.0 * prod_f).astype(BF16)
    const = jnp.sum(mean_f * prod_f - jnp.log(prec_f), axis=1, keepdims=True)
    nt = (((1,), (1,)), ((), ()))

    def rescore(f, ch):
        @pl.loop(0, 4)
        def _(t):
            r = pl.ds(pl.multiple_of(t * 512, 512), 512)
            qt = lax.dot_general(prec_b, sq[f, ch, r, :], nt, preferred_element_type=F32)
            qt += lax.dot_general(minus2, xs[f, ch, r, :], nt, preferred_element_type=F32)
            v = jnp.sum((qt + const) * post[f, ch, :, r].astype(F32), axis=0, keepdims=True)
            for i in range(4):
                s = t * 4 + i
                qb[ch, s if f == 0 else rev4(s), f : f + 1, :] = v[:, i * 128 : (i + 1) * 128]

    rescore(0, 1 - c)
    rescore(1, 1 - c)

    def q_copy(i, src, dst, dev):
        return pltpu.make_async_remote_copy(
            src_ref=src, dst_ref=dst, send_sem=q_s.at[i], recv_sem=q_r.at[i],
            device_id={"states": dev}, device_id_type=MESH,
        )

    q_copies = [q_copy(0, qb.at[1 - c], rq, core)]
    q_copies[0].start()
    o_step(0)
    rescore(0, c)
    o_step(1)
    rescore(1, c)
    q_copies[0].wait_recv()
    summed = qb[c] + rq[...]
    qb[c] = summed
    bits = (v3, v2, v1, v0)
    dims = (3, 2, 1, 0)
    srcs = (qb.at[c], q8, q4, q2)
    sums = (q8, q4, q2, q1)
    recvs = (r8, r4, r2, r1)
    for i in range(4):
        n = 8 >> i
        b = bits[i]
        cp = q_copy(i + 1, srcs[i].at[pl.ds((1 - b) * n, n)], recvs[i], near[dims[i]])
        cp.start()
        q_copies.append(cp)
        if i == 1:
            o_step(2)
        cp.wait_recv()
        sums[i][...] = srcs[i][pl.ds(b * n, n)] + recvs[i][...]

    def h_copy(d):
        return pltpu.make_async_remote_copy(
            src_ref=q1, dst_ref=rh.at[d - 1], send_sem=h_s.at[d - 1], recv_sem=h_r.at[d - 1],
            device_id={"frames": (hi + d) % 4}, device_id_type=MESH,
        )

    for d in range(1, 4):
        h_copy(d).start()
    for d in range(1, 4):
        h_copy(d).wait_recv()
    quad = q1[0] + rh[0, 0] + rh[1, 0] + rh[2, 0]
    w_sum = jnp.sum(w_t, axis=0, keepdims=True)
    for f in range(2):
        score_ref[f : f + 1, :] = -0.5 * quad[f : f + 1, :] / (D * w_sum[:, f * 128 : (f + 1) * 128])

    o_step(3)
    for k in range(-1, 4):
        for t in range(2):
            of[t].arrive_core(k)

    gf.finish()
    for f in range(2):
        xf[f].finish()
        of[f].finish()
        acc_copy(f).wait_send()
        for cp in up_copies(f, z):
            cp.wait_send()
    for cp in q_copies:
        cp.wait_send()
    for d in range(1, 4):
        h_copy(d).wait_send()


def per_device(features, state_ids, weights):
    vm = pl.BlockSpec(memory_space=pltpu.VMEM)
    dma = pltpu.SemaphoreType.DMA
    states = 64 * ROWS
    means, precs, score = pl.pallas_call(
        kernel,
        out_shape=(
            jax.ShapeDtypeStruct((states, W), BF16),
            jax.ShapeDtypeStruct((states, W), BF16),
            jax.ShapeDtypeStruct((2, 128), F32),
        ),
        in_specs=[vm] * 3,
        out_specs=(vm,) * 3,
        scratch_shapes=[
            pltpu.VMEM((2, 2, 2048, W), BF16),
            pltpu.VMEM((2, 2, 2048, W), BF16),
            pltpu.VMEM((2, 16, 64, 256), I16),
            pltpu.VMEM((2, 2, 2 * ROWS, 2048), BF16),
            pltpu.VMEM((2 * ROWS, 640), F32),
            pltpu.VMEM((2, OWN, 640), F32),
            pltpu.VMEM((2, 16, 2, 128), F32),
            pltpu.VMEM((16, 2, 128), F32),
            *[pltpu.VMEM((n, 2, 128), F32) for n in (8, 4, 2, 1)],
            *[pltpu.VMEM((n, 2, 128), F32) for n in (8, 4, 2, 1)],
            pltpu.VMEM((3, 1, 2, 128), F32),
            dma((21, 1)), dma((21, 1)),
            dma((2, 21, 1)), dma((2, 21, 1)),
            dma((2, 21, 2)), dma((2, 21, 2)),
            dma((6,)), dma((6,)),
            dma((5,)), dma((5,)),
            dma((3,)), dma((3,)),
        ],
        compiler_params=pltpu.CompilerParams(
            collective_id=0, has_side_effects=True, vmem_limit_bytes=60 << 20
        ),
        name="fused",
    )(features, state_ids, weights)
    return means, precs, score.reshape(-1)


def solution(mesh):
    return jax.shard_map(
        per_device,
        mesh=mesh,
        in_specs=(P("states", "frames"), P("states", None), P("states", None)),
        out_specs=(P(None, "frames"), P(None, "frames"), P("states")),
        check_vma=False,
    )
```

time: 358 us -> 90.1 us (0.25)
  waiting for transfers between devices: 127 us -> 0 us
  Pallas kernels: 0 us -> 80 us
  other arithmetic: 75.8 us -> 0 us
  blocking collectives: 66.1 us -> 0 us
  local copies, waits for them, and re-layouts: 63.5 us -> 9.17 us
  between operations: 14.2 us -> 0.65 us
  matrix products: 10.4 us -> 0 us
    all_gather x2 -> x0, waiting for transfers between devices: 127 us -> none  [the longest x1 108 us: per_device(): lax.all_gather(jnp.concatenate([mean_rows, prec_rows], axis=1), 'states',...]
    pallas_call x0 -> x1, Pallas kernels: none -> 80 us  [per_device(): pl.pallas_call(kernel, out_shape=(jax.ShapeDtypeStruct((states, W), BF16)...]
    all_to_all x2 -> x0, blocking collectives: 66.1 us -> none  [the longest x1 53.7 us: per_device(): lax.all_to_all(blocked, 'states', split_axis=1, concat_axis=0, tiled=True)]
    unnamed x4 -> x0, other arithmetic: 59.3 us -> none
    gather x2 -> x0, local copies, waits for them, and re-layouts: 45.6 us -> none  [per_device(): quadratic = quadratic + jnp.sum(weight_f * constant_term[state_ids], axis=1)]
    reshape x2 -> x0, local copies, waits for them, and re-layouts: 10.5 us -> none  [per_device(): blocked = posterior.reshape(rows_here, group_size, STATE_DEV)]
    dot_general x2 -> x0, matrix products: 10.4 us -> none  [the longest x1 8.54 us: per_device(): lax.dot_general(routed, joined, (((0,), (0,)), ((), ())), preferred_eleme...]
    convert_element_type x2 -> x0, other arithmetic: 8.82 us -> none  [the longest x1 8.71 us: per_device(): piece_sq = (piece_f * piece_f).astype(jnp.bfloat16)]
  transfers between devices with their start and end apart: 2 -> 0, of which waited for: 2 -> 0; matrix products, arithmetic and copies ran while one was open for 22% -> 0% of each run, Pallas kernels for 0% -> 0%
where the time goes in v1:
time: 90.1 us; the launch traced here: 89.8 us
  Pallas kernels  80 us (89%)
  local copies, waits for them, and re-layouts  9.17 us (10%)
    pallas_call x1, Pallas kernels, per_device(): pl.pallas_call(kernel, out_shape=(jax.ShapeDtypeStruct((states, W), BF16)...  80 us
    unnamed x9, local copies, waits for them, and re-layouts  9.17 us

profile of v1, /device:TPU:1, one launch (start us, length us, event | category | flops | bytes accessed | tf_op | source)
XLA Modules:
  0.0 89.8 jit_solution(7298713106975938696)
XLA Ops:
  0.6 1.5 %copy.6.ids_ref = s32[256,32]{1,0:T(8,128)} copy(s32[256,32]{0,1:T(8,128)} %param.4) | data formatting | bytes 65536 | tf_op args[1]
  2.1 1.5 %copy.7.w_ref = f32[256,32]{1,0:T(8,128)} copy(f32[256,32]{0,1:T(8,128)} %param.5) | data formatting | bytes 65536 | tf_op args[2]
  3.7 80.0 %fused.1 = (bf16[6144,256]{1,0:T(8,128)(2,1)}, bf16[6144,256]{1,0:T(8,128)(2,1)}, f32[2,128]{1,0:T(2,128)}) custom-call(bf16[256,256]{1,0:T(8,128)(2,1)} %x_ref.1, s32[256,32]{1,0:T(8,128)} %copy.6.ids_ref, f32[256,32]{1,0:T(8,128)} %copy.7.w_ref), custom_call_target="tpu_custom_call" | custom-call | tf_op jit(solution)/shard_map/fused/pallas_call | solution.py:374
  83.7 0.0 copy-start
  83.7 3.9 %copy.11 = bf16[6144,256]{1,0:T(8,128)(2,1)} copy(bf16[6144,256]{1,0:T(8,128)(2,1)} %get-tuple-element.12) | data formatting | bytes 6291456
  87.6 0.0 copy-done
  87.6 0.0 copy-start.1
  87.6 1.7 %copy.12 = bf16[6144,256]{1,0:T(8,128)(2,1)} copy(bf16[6144,256]{1,0:T(8,128)(2,1)S(1)} %copy-done) | data formatting | bytes 6291456
  89.3 0.0 copy-done.1
  89.3 0.6 copy.13
Async XLA Ops:
  83.7 3.9 %copy-start = (bf16[6144,256]{1,0:T(8,128)(2,1)S(1)}, bf16[6144,256]{1,0:T(8,128)(2,1)}, u32[]{:S(2)}) copy-start(bf16[6144,256]{1,0:T(8,128)(2,1)} %get-tuple-element.13) | copy-start | bytes 9437188
  87.6 1.7 %copy-start.1 = (f32[2,128]{1,0:T(2,128)S(1)}, f32[2,128]{1,0:T(2,128)}, u32[]{:S(2)}) copy-start(f32[2,128]{1,0:T(2,128)} %get-tuple-element.8) | copy-start | bytes 3076

commit v2 on v1

v2 whole, which is shorter than its diff:
```python
import jax
import jax.numpy as jnp
from jax import lax
from jax.experimental import pallas as pl
from jax.experimental.pallas import tpu as pltpu
from jax.sharding import PartitionSpec as P

MESH = pl.DeviceIdType.MESH
F32, BF16, I16, I32 = jnp.float32, jnp.bfloat16, jnp.int16, jnp.int32
D = 1024
W = 256
ROWS = 96
OWN = 48
FLOOR = 0.25
HOPS = ((0,), (1, 2, 4, 8), (3, 5, 6, 9, 10, 12), (7, 11, 13, 14), (15,))


def flip(s, mask):
    for k in range(4):
        if mask >> k & 1:
            s = s + 2**k * (1 - 2 * ((s // 2**k) % 2))
    return s


def rev4(s):
    return (s % 2) * 8 + ((s // 2) % 2) * 4 + ((s // 4) % 2) * 2 + s // 8


def gray(r):
    return (r + r // 2) % 2 + 2 * (r // 2)


class Flood:
    def __init__(self, views, ssem, rsem, slot, slot_other, partners, core, c):
        self.views, self.ssem, self.rsem = views, ssem, rsem
        self.slot, self.slot_other, self.partners, self.core, self.c = slot, slot_other, partners, core, c

    def _copies(self, region, s, i, device):
        return [
            pltpu.make_async_remote_copy(
                src_ref=view(region, s), dst_ref=view(region, s), send_sem=self.ssem.at[i, a],
                recv_sem=self.rsem.at[i, a], device_id={"states": device}, device_id_type=MESH,
            )
            for a, view in enumerate(self.views)
        ]

    def _out(self, m, k):
        return self._copies(self.c, flip(self.slot, m), m | 1 << k, self.partners[k])

    def _in(self, m):
        return self._copies(self.c, flip(self.slot, m), m, self.partners[m.bit_length() - 1])

    def _core_out(self, m):
        return self._copies(self.c, flip(self.slot, m), 16 + m, self.core)

    def _core_in(self, m):
        return self._copies(1 - self.c, flip(self.slot_other, m), 16 + m, self.core)

    def spread(self, m):
        for k in range(m.bit_length(), 4):
            for cp in self._out(m, k):
                cp.start()
        for cp in self._core_out(m):
            cp.start()

    def arrive(self, m):
        for cp in self._in(m):
            cp.wait_recv()
        self.spread(m)

    def arrive_core(self, m):
        for cp in self._core_in(m):
            cp.wait_recv()

    def finish(self):
        for m in range(16):
            for k in range(m.bit_length(), 4):
                for cp in self._out(m, k):
                    cp.wait_send()
            for cp in self._core_out(m):
                cp.wait_send()


def kernel(
    x_hbm, ids_hbm, w_hbm, om_ref, op_ref, score_ref,
    x_in, ids_in, w_in, xs, sq, g, post, acc, racc, occ, oc, roc, cnt, qb, rq, qy, ry, qx, rx, q1, rh,
    i_s, g_s, g_r, x_s, x_r, o_s, o_r, z_s, z_r, q_s, q_r, h_s, h_r,
):
    me = lax.axis_index("states")
    hi = lax.axis_index("frames")
    c = me % 2
    x = (me // 2) % 4
    y = (me // 8) % 4
    z = me // 32

    def device(z, y, x, c):
        return ((z * 4 + y) * 4 + x) * 2 + c

    p = x + c * (y - x)
    q = y + c * (x - y)

    def at(p2, q2):
        return device(z, q2 + c * (p2 - q2), p2 + c * (q2 - p2), c)

    v0, v1, v2, v3 = (p + p // 2) % 2, p // 2, (q + q // 2) % 2, q // 2
    near = [at(p + 1 - 2 * (p % 2), q), at(3 - p, q), at(p, q + 1 - 2 * (q % 2)), at(p, 3 - q)]
    core = device(z, y, x, 1 - c)
    up = device(1 - z, y, x, c)
    slot = (v0 + 2 * v1 + 4 * v2 + 8 * v3, v3 + 2 * v2 + 4 * v1 + 8 * v0)
    other = (v2 + 2 * v3 + 4 * v0 + 8 * v1, v1 + 2 * v0 + 4 * v3 + 8 * v2)

    barrier = pltpu.get_barrier_semaphore()
    for d in near + [at((p + 2) % 4, q), at(p, (q + 2) % 4), core, up]:
        pl.semaphore_signal(barrier, inc=1, device_id={"states": d}, device_id_type=MESH)
    for d in range(1, 4):
        pl.semaphore_signal(barrier, inc=1, device_id={"frames": (hi + d) % 4}, device_id_type=MESH)

    loads = [
        pltpu.make_async_copy(src, dst, i_s.at[i])
        for i, (src, dst) in enumerate(((ids_hbm, ids_in), (w_hbm, w_in), (x_hbm, x_in)))
    ]
    for cp in loads:
        cp.start()
    acc[...] = jnp.zeros_like(acc)
    occ[...] = jnp.zeros_like(occ)
    loads[0].wait()
    loads[1].wait()
    w_t = w_in[...].astype(BF16).astype(F32)
    g[c, slot[0], 0:32, :] = ids_in[...].astype(I16)
    g[c, slot[0], 32:64, :] = (w_t * 4096.0).astype(I32).astype(I16)
    loads[2].wait()
    for f in range(2):
        xs[f, c, pl.ds(pl.multiple_of(slot[f] * 128, 128), 128), :] = x_in[f * 128 : (f + 1) * 128, :]

    base = [pl.multiple_of(((c * 2 + part) * 16 + slot[part]) * ROWS, ROWS) for part in range(2)]
    iota = lax.broadcasted_iota(I32, (ROWS, 128), 0)
    rows = jnp.concatenate([(iota + base[0]).astype(I16), (iota + base[1]).astype(I16)], axis=0)

    def build(ch, s):
        ids = g[ch, s, 0:32, :].astype(I32)
        wv = g[ch, s, 32:64, :].astype(I32).astype(F32) * (1.0 / 4096.0)
        for f in range(2):
            lanes = slice(f * 128, (f + 1) * 128)
            block = jnp.zeros((2 * ROWS, 128), BF16)
            for j in range(32):
                idj = jnp.broadcast_to(ids[j : j + 1, lanes].astype(I16), (2 * ROWS, 128))
                wj = jnp.broadcast_to(wv[j : j + 1, lanes].astype(BF16), (2 * ROWS, 128))
                block = jnp.where(rows == idj, wj, block)
            col = pl.multiple_of((s if f == 0 else rev4(s)) * 128, 128)
            post[f, ch, :, pl.ds(col, 128)] = block
            occ[...] += block.astype(F32)

    def build_all(ch, first, h):
        def body(_, left):
            s = first
            for k in range(4):
                s = s + 2**k * ((left // 2**k) % 2) * (1 - 2 * ((first // 2**k) % 2))
            build(ch, s)
            return left // 16

        lax.fori_loop(0, len(HOPS[h]), body, jnp.int32(sum(m << 4 * i for i, m in enumerate(HOPS[h]))))

    def moments(f, ch, b):
        r = pl.ds(pl.multiple_of(b * 512, 512), 512)
        xv = xs[f, ch, r, :]
        xw = xv.astype(F32)
        sv = (xw * xw).astype(BF16)
        sq[f, ch, r, :] = sv
        pv = post[f, ch, :, r]
        acc[:, 0:256] += jnp.dot(pv, xv, preferred_element_type=F32)
        acc[:, 256:512] += jnp.dot(pv, sv, preferred_element_type=F32)

    def g_view(r, s):
        return g.at[r, s]

    def x_view(f):
        return lambda r, s: xs.at[f, r, pl.ds(pl.multiple_of(s * 128, 128), 128)]

    orders = (near, near[::-1])
    gf = Flood([g_view], g_s, g_r, slot[0], other[0], near, core, c)
    xf = [Flood([x_view(f)], x_s.at[f], x_r.at[f], slot[f], other[f], orders[f], core, c) for f in range(2)]

    def g_hop(h):
        for m in HOPS[h]:
            gf.arrive(m)

    def g_core(h):
        for m in HOPS[h]:
            gf.arrive_core(m)

    def x_hop(h):
        for m in HOPS[h]:
            for f in range(2):
                xf[f].arrive(m)

    def x_core(h):
        for m in HOPS[h]:
            for f in range(2):
                xf[f].arrive_core(m)

    with jax.named_scope("a0_barrier"):
        pl.semaphore_wait(barrier, 11)
    gf.spread(0)
    with jax.named_scope("b0_build"):
        build(c, slot[0])
    with jax.named_scope("b1_gcore0"):
        g_core(0)
        build(1 - c, other[0])
    with jax.named_scope("b2_ghop1"):
        g_hop(1)
    for f in range(2):
        xf[f].spread(0)
    with jax.named_scope("b3_build"):
        build_all(c, slot[0], 1)
    with jax.named_scope("b4_gcore1"):
        g_core(1)
    with jax.named_scope("b5_build"):
        build_all(1 - c, other[0], 1)
    with jax.named_scope("b6_ghop2"):
        g_hop(2)
    with jax.named_scope("b7_xhop1"):
        x_hop(1)
    with jax.named_scope("b8_build"):
        build_all(c, slot[0], 2)
    with jax.named_scope("c0_ghop3"):
        g_hop(3)
    with jax.named_scope("c1_gcore2"):
        g_core(2)
    with jax.named_scope("c2_build"):
        build_all(1 - c, other[0], 2)
    with jax.named_scope("c3_xhop2"):
        x_hop(2)
    with jax.named_scope("c4_ghop4"):
        g_hop(4)
    with jax.named_scope("c5_build"):
        build_all(c, slot[0], 3)
    with jax.named_scope("c6_gcore3"):
        g_core(3)
    with jax.named_scope("c7_build"):
        build_all(1 - c, other[0], 3)
    with jax.named_scope("c8_xhop3"):
        x_hop(3)
    with jax.named_scope("c9_build"):
        build(c, flip(slot[0], 15))
        g_core(4)
        build(1 - c, flip(other[0], 15))

    oc[...] = jnp.zeros_like(oc)
    oc[0:1, 0:192] = jnp.sum(jnp.transpose(occ[...]), axis=0, keepdims=True)

    def up_copy(i, src, dst):
        return pltpu.make_async_remote_copy(
            src_ref=src, dst_ref=dst, send_sem=z_s.at[i], recv_sem=z_r.at[i],
            device_id={"states": up}, device_id_type=MESH,
        )

    oc_copy = up_copy(6, oc, roc)
    oc_copy.start()

    def quarter(s, mask):
        return flip(s, mask) // 4

    with jax.named_scope("d0_xcore"):
        for h in range(3):
            x_core(h)
    with jax.named_scope("d1_mom"):
        for mask in (0, 4, 8):
            if mask == 4:
                x_core(3)
            for f in range(2):
                moments(f, c, quarter(slot[f], mask))
                moments(f, 1 - c, quarter(other[f], mask))
    with jax.named_scope("d2_xhop4"):
        x_hop(4)
    with jax.named_scope("d3_mom"):
        for f in range(2):
            moments(f, c, quarter(slot[f], 12))
    with jax.named_scope("d4_xcore4"):
        x_core(4)
    with jax.named_scope("d5_mom"):
        for f in range(2):
            moments(f, 1 - c, quarter(other[f], 12))

    def acc_copy(part):
        return up_copy(part, acc.at[pl.ds(pl.multiple_of(part * ROWS + (1 - z) * OWN, 8), OWN)], racc.at[part])

    def own_rows(part, zz):
        return pl.ds(pl.multiple_of(base[part] + zz * OWN, 16), OWN)

    def up_copies(part, zz):
        return [
            up_copy(2 + part * 2 + a, ref.at[own_rows(part, zz)], ref.at[own_rows(part, zz)])
            for a, ref in enumerate((om_ref, op_ref))
        ]

    for part in range(2):
        acc_copy(part).start()
    oc_copy.wait_recv()
    cnt[...] = jnp.transpose(jnp.broadcast_to(oc[0:1, :] + roc[0:1, :], (128, 256)))
    for part in range(2):
        with jax.named_scope("e0_accwait"):
            acc_copy(part).wait_recv()
        mine = pl.ds(pl.multiple_of(part * ROWS + z * OWN, 8), OWN)
        total = acc[mine, :] + racc[part]
        count = jnp.concatenate([cnt[mine, :], cnt[mine, :]], axis=1)
        mean = total[:, 0:256] / count
        var = jnp.maximum(total[:, 256:512] / count - mean * mean, FLOOR)
        om_ref[own_rows(part, z), :] = mean.astype(BF16)
        op_ref[own_rows(part, z), :] = (1.0 / var).astype(BF16)
        for cp in up_copies(part, z):
            cp.start()

    def o_view(ref, part):
        def view(r, s):
            return ref.at[pl.ds(pl.multiple_of(((r * 2 + part) * 16 + s) * ROWS, ROWS), ROWS)]
        return view

    of = [
        Flood([o_view(om_ref, t), o_view(op_ref, t)], o_s.at[t], o_r.at[t], slot[t], other[t], orders[t], core, c)
        for t in range(2)
    ]
    for part in range(2):
        with jax.named_scope("e1_upwait"):
            for cp in up_copies(part, 1 - z):
                cp.wait_recv()
        of[part].spread(0)

    def o_hop(h):
        for m in HOPS[h]:
            for t in range(2):
                of[t].arrive(m)

    both = [pl.ds(base[part], ROWS) for part in range(2)]
    mean_b = jnp.concatenate([om_ref[r, :] for r in both], axis=0)
    prec_b = jnp.concatenate([op_ref[r, :] for r in both], axis=0)
    mean_f, prec_f = mean_b.astype(F32), prec_b.astype(F32)
    prod_f = (mean_f * prec_f).astype(BF16).astype(F32)
    minus2 = (-2.0 * prod_f).astype(BF16)
    const = jnp.sum(mean_f * prod_f - jnp.log(prec_f), axis=1, keepdims=True)
    nt = (((1,), (1,)), ((), ()))

    def rescore(f, ch):
        @pl.loop(0, 4)
        def _(t):
            r = pl.ds(pl.multiple_of(t * 512, 512), 512)
            qt = lax.dot_general(prec_b, sq[f, ch, r, :], nt, preferred_element_type=F32)
            qt += lax.dot_general(minus2, xs[f, ch, r, :], nt, preferred_element_type=F32)
            v = jnp.sum((qt + const) * post[f, ch, :, r].astype(F32), axis=0, keepdims=True)
            for i in range(4):
                s = t * 4 + i
                qb[ch, s if f == 0 else rev4(s), f : f + 1, :] = v[:, i * 128 : (i + 1) * 128]

    def q_copy(i, src, dst, dev):
        return pltpu.make_async_remote_copy(
            src_ref=src, dst_ref=dst, send_sem=q_s.at[i], recv_sem=q_r.at[i],
            device_id={"states": dev}, device_id_type=MESH,
        )

    with jax.named_scope("f0_rescore"):
        rescore(0, 1 - c)
        rescore(1, 1 - c)
    q_core = q_copy(0, qb.at[1 - c], rq, core)
    q_core.start()
    with jax.named_scope("f1_rescore"):
        rescore(0, c)
        rescore(1, c)
    with jax.named_scope("f2_qcore"):
        q_core.wait_recv()
    qy[...] = qb[c] + rq[...]
    q_y = [q_copy(d, qy.at[pl.ds(gray((q + d) % 4) * 4, 4)], ry.at[d - 1], at(p, (q + d) % 4)) for d in range(1, 4)]
    for cp in q_y:
        cp.start()
    with jax.named_scope("f3_ohop1"):
        o_hop(1)
    with jax.named_scope("f4_qy"):
        for cp in q_y:
            cp.wait_recv()
    qx[...] = qy[pl.ds(gray(q) * 4, 4)] + ry[0] + ry[1] + ry[2]
    q_x = [q_copy(3 + d, qx.at[pl.ds(gray((p + d) % 4), 1)], rx.at[d - 1], at((p + d) % 4, q)) for d in range(1, 4)]
    for cp in q_x:
        cp.start()
    with jax.named_scope("f5_ohop2"):
        o_hop(2)
    with jax.named_scope("f6_qx"):
        for cp in q_x:
            cp.wait_recv()
    q1[...] = qx[pl.ds(gray(p), 1)] + rx[0] + rx[1] + rx[2]

    def h_copy(d):
        return pltpu.make_async_remote_copy(
            src_ref=q1, dst_ref=rh.at[d - 1], send_sem=h_s.at[d - 1], recv_sem=h_r.at[d - 1],
            device_id={"frames": (hi + d) % 4}, device_id_type=MESH,
        )

    for d in range(1, 4):
        h_copy(d).start()
    with jax.named_scope("g0_ohop3"):
        o_hop(3)
    with jax.named_scope("g1_h"):
        for d in range(1, 4):
            h_copy(d).wait_recv()
    quad = q1[0] + rh[0, 0] + rh[1, 0] + rh[2, 0]
    w_sum = jnp.sum(w_t, axis=0, keepdims=True)
    for f in range(2):
        score_ref[f : f + 1, :] = -0.5 * quad[f : f + 1, :] / (D * w_sum[:, f * 128 : (f + 1) * 128])
    with jax.named_scope("g2_ohop4"):
        o_hop(4)
    with jax.named_scope("g3_ocore"):
        for m in range(16):
            for t in range(2):
                of[t].arrive_core(m)

    with jax.named_scope("g4_finish"):
        gf.finish()
        oc_copy.wait_send()
        q_core.wait_send()
        for f in range(2):
            xf[f].finish()
            of[f].finish()
            acc_copy(f).wait_send()
            for cp in up_copies(f, z):
                cp.wait_send()
        for cp in q_y + q_x:
            cp.wait_send()
        for d in range(1, 4):
            h_copy(d).wait_send()


def per_device(features, state_ids, weights):
    hbm = pl.BlockSpec(memory_space=pl.ANY)
    vm = pl.BlockSpec(memory_space=pltpu.VMEM)
    dma = pltpu.SemaphoreType.DMA
    states = 64 * ROWS
    means, precs, score = pl.pallas_call(
        kernel,
        out_shape=(
            pltpu.VMEM((states, W), BF16),
            pltpu.VMEM((states, W), BF16),
            pltpu.VMEM((2, 128), F32),
        ),
        in_specs=[hbm] * 3,
        out_specs=(vm,) * 3,
        scratch_shapes=[
            pltpu.VMEM((256, W), BF16),
            pltpu.VMEM((32, 256), I32),
            pltpu.VMEM((32, 256), F32),
            pltpu.VMEM((2, 2, 2048, W), BF16),
            pltpu.VMEM((2, 2, 2048, W), BF16),
            pltpu.VMEM((2, 16, 64, 256), I16),
            pltpu.VMEM((2, 2, 2 * ROWS, 2048), BF16),
            pltpu.VMEM((2 * ROWS, 512), F32),
            pltpu.VMEM((2, OWN, 512), F32),
            pltpu.VMEM((2 * ROWS, 128), F32),
            pltpu.VMEM((8, 256), F32),
            pltpu.VMEM((8, 256), F32),
            pltpu.VMEM((256, 128), F32),
            pltpu.VMEM((2, 16, 2, 128), F32),
            pltpu.VMEM((16, 2, 128), F32),
            pltpu.VMEM((16, 2, 128), F32),
            pltpu.VMEM((3, 4, 2, 128), F32),
            pltpu.VMEM((4, 2, 128), F32),
            pltpu.VMEM((3, 1, 2, 128), F32),
            pltpu.VMEM((1, 2, 128), F32),
            pltpu.VMEM((3, 1, 2, 128), F32),
            dma((3,)),
            dma((32, 1)), dma((32, 1)),
            dma((2, 32, 1)), dma((2, 32, 1)),
            dma((2, 32, 2)), dma((2, 32, 2)),
            dma((7,)), dma((7,)),
            dma((7,)), dma((7,)),
            dma((3,)), dma((3,)),
        ],
        compiler_params=pltpu.CompilerParams(
            collective_id=0, has_side_effects=True, vmem_limit_bytes=40 << 20
        ),
        name="fused",
    )(features, state_ids.T, weights.T)
    return means, precs, score.reshape(-1)


def solution(mesh):
    return jax.shard_map(
        per_device,
        mesh=mesh,
        in_specs=(P("states", "frames"), P("states", None), P("states", None)),
        out_specs=(P(None, "frames"), P(None, "frames"), P("states")),
        check_vma=False,
    )
```

time: 90.1 us -> 75.5 us (0.84)
  Pallas kernels: 80 us -> 68.3 us
  local copies, waits for them, and re-layouts: 9.17 us -> 6.31 us
    pallas_call x1, Pallas kernels: 80 us -> 68.3 us  [per_device(): pl.pallas_call(kernel, out_shape=(pltpu.VMEM((states, W), BF16), pltpu.VM...]
    unnamed x9, local copies, waits for them, and re-layouts: 9.17 us -> 6.31 us
where the time goes in v2:
time: 75.5 us; the launch traced here: 75.3 us
  Pallas kernels  68.3 us (90%)
  local copies, waits for them, and re-layouts  6.31 us (8%)
    pallas_call x1, Pallas kernels, per_device(): pl.pallas_call(kernel, out_shape=(pltpu.VMEM((states, W), BF16), pltpu.VM...  68.3 us
    unnamed x9, local copies, waits for them, and re-layouts  6.31 us

profile of v2, /device:TPU:1, one launch (start us, length us, event | category | flops | bytes accessed | tf_op | source)
XLA Modules:
  0.0 75.3 jit_solution(12092957031239934338)
XLA Ops:
  0.6 0.0 copy-start
  0.6 0.9 %copy-done = bf16[256,256]{1,0:T(8,128)(2,1)S(1)} copy-done((bf16[256,256]{1,0:T(8,128)(2,1)S(1)}, bf16[256,256]{1,0:T(8,128)(2,1)}, u32[]{:S(2)}) %copy-start) | copy-done | bytes 131096
  1.5 0.0 copy-start.1
  1.5 0.8 %copy-done.1 = s32[256,32]{0,1:T(8,128)S(1)} copy-done((s32[256,32]{0,1:T(8,128)S(1)}, s32[256,32]{0,1:T(8,128)}, u32[]{:S(2)}) %copy-start.1) | copy-done | bytes 32792
  2.3 0.0 copy-start.2
  2.3 0.8 %copy-done.2 = f32[256,32]{0,1:T(8,128)S(1)} copy-done((f32[256,32]{0,1:T(8,128)S(1)}, f32[256,32]{0,1:T(8,128)}, u32[]{:S(2)}) %copy-start.2) | copy-done | bytes 32792
  3.1 68.3 %fused.1 = (bf16[6144,256]{1,0:T(8,128)(2,1)S(1)}, bf16[6144,256]{1,0:T(8,128)(2,1)S(1)}, f32[2,128]{1,0:T(2,128)S(1)}) custom-call(bf16[256,256]{1,0:T(8,128)(2,1)S(1)} %copy-done, s32[32,256]{1,0:T(8,128)S(1)} %bitcast.4, f32[32,256]{1,0:T(8,128)S(1)} %bitcast.5), custom_call_target="tpu_custom_call" | custom-call | tf_op jit(solution)/shard_map/fused/pallas_call | solution.py:434
  71.4 1.7 %copy.9 = bf16[6144,256]{1,0:T(8,128)(2,1)} copy(bf16[6144,256]{1,0:T(8,128)(2,1)S(1)} %get-tuple-element.9) | data formatting | bytes 6291456
  73.0 0.6 copy.11
  73.6 1.7 %copy.10 = bf16[6144,256]{1,0:T(8,128)(2,1)} copy(bf16[6144,256]{1,0:T(8,128)(2,1)S(1)} %get-tuple-element.10) | data formatting | bytes 6291456
Async XLA Ops:
  0.6 0.9 %copy-start = (bf16[256,256]{1,0:T(8,128)(2,1)S(1)}, bf16[256,256]{1,0:T(8,128)(2,1)}, u32[]{:S(2)}) copy-start(bf16[256,256]{1,0:T(8,128)(2,1)} %x_hbm.1) | copy-start | bytes 393220
  1.5 0.8 %copy-start.1 = (s32[256,32]{0,1:T(8,128)S(1)}, s32[256,32]{0,1:T(8,128)}, u32[]{:S(2)}) copy-start(s32[256,32]{0,1:T(8,128)} %param.4) | copy-start | bytes 98308
  2.3 0.8 %copy-start.2 = (f32[256,32]{0,1:T(8,128)S(1)}, f32[256,32]{0,1:T(8,128)}, u32[]{:S(2)}) copy-start(f32[256,32]{0,1:T(8,128)} %param.5) | copy-start | bytes 98308

commit v3 on v2

v3 whole, which is shorter than its diff:
```python
import jax
import jax.numpy as jnp
from jax import lax
from jax.experimental import pallas as pl
from jax.experimental.pallas import tpu as pltpu
from jax.sharding import PartitionSpec as P

MESH = pl.DeviceIdType.MESH
F32, BF16, I16, I32 = jnp.float32, jnp.bfloat16, jnp.int16, jnp.int32
D = 1024
W = 256
ROWS = 96
OWN = 48
LATE = 32
FLOOR = 0.25
HOPS = ((0,), (1, 2, 4, 8), (3, 5, 6, 9, 10, 12), (7, 11, 13, 14), (15,))
GROUPS = ((1, 2), (4, 8), (3, 5, 6), (9, 10, 12), (7, 11, 13, 14), (15,))
LATER = ((1, 2, 4, 8), (3, 5, 6, 9, 10, 12), (7, 11, 13, 14, 15))


def flip(s, mask):
    for k in range(4):
        if mask >> k & 1:
            s = s + 2**k * (1 - 2 * ((s // 2**k) % 2))
    return s


def rev4(s):
    return (s % 2) * 8 + ((s // 2) % 2) * 4 + ((s // 4) % 2) * 2 + s // 8


def gray(r):
    return (r + r // 2) % 2 + 2 * (r // 2)


def place_of(groups, m):
    return [n for n, group in enumerate(groups) if m in group][0]


def landed(ref, sem):
    pltpu.make_async_copy(ref, ref, sem).wait()


def push(src, dst, send, recv, device):
    return pltpu.make_async_remote_copy(
        src_ref=src, dst_ref=dst, send_sem=send, recv_sem=recv, device_id=device, device_id_type=MESH
    )


class Flood:
    def __init__(self, view, slot, partners, core, c, send, recv, core_recv, first=None, up=None, up_view=None, up_recv=None):
        self.view, self.slot, self.partners, self.core, self.c = view, slot, partners, core, c
        self.send, self.recv, self.core_recv, self.first = send, recv, core_recv, first
        self.up, self.up_view, self.up_recv = up, up_view, up_recv

    def _pass(self, m, view, recv, device):
        dst = view(self.c, flip(self.slot, m))
        src = self.first if m == 0 and self.first is not None else dst
        push(src, dst, self.send, recv, {"states": device}).start()

    def start(self, ks):
        for k in ks:
            self._pass(0, self.view, self.recv(1 << k), self.partners[k])

    def start_core(self):
        self._pass(0, self.view, self.core_recv(0), self.core)

    def forward(self, m):
        for k in range(m.bit_length(), 4):
            self._pass(m, self.view, self.recv(m | 1 << k), self.partners[k])
        if self.up_view:
            self._pass(m, self.up_view, self.up_recv(m), self.up)
        self._pass(m, self.view, self.core_recv(m), self.core)


def kernel(
    x_hbm, ids_hbm, w_hbm, out, score_ref,
    x_in, ids_in, w_in, xs, g, post, acc, racc, occ, oc, roc, cnt, tb, qb, rq, qy, ry, qx, rx, q1, rh,
    i_s, g_s, g_r, g_c, x_s, x_r, x_c, o_s, o_r, t_r, u_r, o_c, acc_s, acc_r, tb_s, tb_r, oc_s, oc_r, l_s, q_s, q_r,
):
    me = lax.axis_index("states")
    hi = lax.axis_index("frames")
    c = me % 2
    x = (me // 2) % 4
    y = (me // 8) % 4
    z = me // 32

    def device(z, y, x, c):
        return ((z * 4 + y) * 4 + x) * 2 + c

    p = x + c * (y - x)
    q = y + c * (x - y)

    def at(p2, q2):
        return device(z, q2 + c * (p2 - q2), p2 + c * (q2 - p2), c)

    v0, v1, v2, v3 = (p + p // 2) % 2, p // 2, (q + q // 2) % 2, q // 2
    near = [at(p + 1 - 2 * (p % 2), q), at(3 - p, q), at(p, q + 1 - 2 * (q % 2)), at(p, 3 - q)]
    core = device(z, y, x, 1 - c)
    up = device(1 - z, y, x, c)
    slot = (v0 + 2 * v1 + 4 * v2 + 8 * v3, v3 + 2 * v2 + 4 * v1 + 8 * v0)
    other = (v2 + 2 * v3 + 4 * v0 + 8 * v1, v1 + 2 * v0 + 4 * v3 + 8 * v2)

    barrier = pltpu.get_barrier_semaphore()
    for d in near + [at((p + 2) % 4, q), at(p, (q + 2) % 4), core, up]:
        pl.semaphore_signal(barrier, inc=1, device_id={"states": d}, device_id_type=MESH)
    for d in range(1, 4):
        pl.semaphore_signal(barrier, inc=1, device_id={"frames": (hi + d) % 4}, device_id_type=MESH)

    loads = [
        pltpu.make_async_copy(src, dst, i_s.at[i])
        for i, (src, dst) in enumerate(((ids_hbm, ids_in), (w_hbm, w_in), (x_hbm, x_in)))
    ]
    for cp in loads:
        cp.start()
    acc[...] = jnp.zeros_like(acc)
    occ[...] = jnp.zeros_like(occ)
    loads[0].wait()
    loads[1].wait()
    w_t = w_in[...].astype(BF16).astype(F32)
    g[c * 16 + slot[0], 0:32, :] = ids_in[...].astype(I16)
    g[c * 16 + slot[0], 32:64, :] = (w_t * 4096.0).astype(I32).astype(I16)
    loads[2].wait()
    for f in range(2):
        xs[f, c, pl.ds(pl.multiple_of(slot[f] * 128, 128), 128), 0:W] = x_in[f * 128 : (f + 1) * 128, :]

    base = [pl.multiple_of(((c * 2 + part) * 16 + slot[part]) * ROWS, ROWS) for part in range(2)]
    iota = lax.broadcasted_iota(I32, (ROWS, 128), 0)
    rows = jnp.concatenate([(iota + base[0]).astype(I16), (iota + base[1]).astype(I16)], axis=0)

    def build(ch, s):
        ids = g[ch * 16 + s, 0:32, :].astype(I32)
        wv = g[ch * 16 + s, 32:64, :].astype(I32).astype(F32) * (1.0 / 4096.0)
        for f in range(2):
            lanes = slice(f * 128, (f + 1) * 128)
            block = jnp.zeros((2 * ROWS, 128), BF16)
            for j in range(32):
                idj = jnp.broadcast_to(ids[j : j + 1, lanes].astype(I16), (2 * ROWS, 128))
                wj = jnp.broadcast_to(wv[j : j + 1, lanes].astype(BF16), (2 * ROWS, 128))
                block = jnp.where(rows == idj, wj, block)
            col = pl.multiple_of((s if f == 0 else rev4(s)) * 128, 128)
            post[f, ch, :, pl.ds(col, 128)] = block
            occ[...] += block.astype(F32)

    def build_all(ch, first, h):
        def body(_, left):
            s = first
            for k in range(4):
                s = s + 2**k * ((left // 2**k) % 2) * (1 - 2 * ((first // 2**k) % 2))
            build(ch, s)
            return left // 16

        lax.fori_loop(0, len(HOPS[h]), body, jnp.int32(sum(m << 4 * i for i, m in enumerate(HOPS[h]))))

    def moments(f, ch, b):
        r = pl.ds(pl.multiple_of(b * 512, 512), 512)
        xw = xs[f, ch, r, 0:W].astype(F32)
        xs[f, ch, r, W : 2 * W] = (xw * xw).astype(BF16)
        acc[...] += jnp.dot(post[f, ch, :, r], xs[f, ch, r, :], preferred_element_type=F32)

    orders = (near, near[::-1])
    gf = Flood(
        lambda r, s: g.at[r * 16 + s], slot[0], near, core, c, g_s.at[0],
        lambda m: g_r.at[place_of(HOPS, m) - 1], lambda m: g_c.at[place_of(HOPS, m)],
    )
    xf = [
        Flood(
            lambda r, s, f=f: xs.at[f, r, pl.ds(pl.multiple_of(s * 128, 128), 128), 0:W], slot[f], orders[f], core, c,
            x_s.at[0], lambda m: x_r.at[place_of(GROUPS, m)], lambda m: x_c.at[max(m.bit_count(), 2) - 2],
        )
        for f in range(2)
    ]

    def g_hop(h):
        landed(g.at[0 : len(HOPS[h])], g_r.at[h - 1])
        for m in HOPS[h]:
            gf.forward(m)

    def g_core(h):
        landed(g.at[0 : len(HOPS[h])], g_c.at[h])

    def x_group(i):
        landed(xs.at[0, 0, 0 : len(GROUPS[i]) * 256, 0:W], x_r.at[i])
        for m in GROUPS[i]:
            for f in range(2):
                xf[f].forward(m)

    def x_core(i):
        landed(xs.at[:, 0, 0 : (11, 4, 1)[i] * 128, 0:W], x_c.at[i])

    def quarter(s, mask):
        return flip(s, mask) // 4

    def own_moments(mask):
        for f in range(2):
            moments(f, c, quarter(slot[f], mask))

    def core_moments(mask):
        for f in range(2):
            moments(f, 1 - c, quarter(other[f], mask))

    with jax.named_scope("a0_barrier"):
        pl.semaphore_wait(barrier, 11)
    gf.start(range(4))
    gf.start_core()
    for ks in ((0, 1), (2, 3)):
        for f in range(2):
            xf[f].start(ks)
    for f in range(2):
        xf[f].start_core()
    with jax.named_scope("b0_build"):
        build(c, slot[0])
    with jax.named_scope("b1_gcore0"):
        g_core(0)
        build(1 - c, other[0])
    with jax.named_scope("b2_ghop1"):
        g_hop(1)
    with jax.named_scope("b3_x12"):
        x_group(0)
    with jax.named_scope("b4_build"):
        build_all(c, slot[0], 1)
    with jax.named_scope("b5_x48"):
        x_group(1)
    with jax.named_scope("b6_gcore1"):
        g_core(1)
        build_all(1 - c, other[0], 1)
    with jax.named_scope("b7_ghop2"):
        g_hop(2)
    with jax.named_scope("b8_build"):
        build_all(c, slot[0], 2)
    with jax.named_scope("c0_x356"):
        x_group(2)
    with jax.named_scope("c1_ghop3"):
        g_hop(3)
    with jax.named_scope("c2_build"):
        g_core(2)
        build_all(1 - c, other[0], 2)
    with jax.named_scope("c3_x9"):
        x_group(3)
    with jax.named_scope("c4_build"):
        build_all(c, slot[0], 3)
    with jax.named_scope("c5_ghop4"):
        g_hop(4)
    with jax.named_scope("c6_build"):
        g_core(3)
        build_all(1 - c, other[0], 3)
    with jax.named_scope("c7_x7"):
        x_group(4)
    with jax.named_scope("c8_build"):
        build(c, flip(slot[0], 15))
        g_core(4)
        build(1 - c, flip(other[0], 15))

    oc[...] = jnp.zeros_like(oc)
    oc[0:1, 0:192] = jnp.sum(jnp.transpose(occ[...]), axis=0, keepdims=True)

    def up_push(src, dst, send, recv):
        return push(src, dst, send, recv, {"states": up})

    up_push(oc, roc, oc_s.at[0], oc_r.at[0]).start()

    with jax.named_scope("d0_mom"):
        own_moments(0)
        x_core(0)
        core_moments(0)
        own_moments(4)
        own_moments(8)
    with jax.named_scope("d1_x15"):
        x_group(5)
    with jax.named_scope("d2_mom"):
        x_core(1)
        core_moments(4)
        core_moments(8)
        own_moments(12)
    with jax.named_scope("d3_xcore4"):
        x_core(2)
    with jax.named_scope("d4_mom"):
        core_moments(12)

    for part in range(2):
        r = pl.ds(pl.multiple_of(part * ROWS + (1 - z) * OWN, 8), OWN)
        up_push(acc.at[r], racc.at[part], acc_s.at[0], acc_r.at[part]).start()

    def rows_of(part, r, s, first, n):
        return out.at[:, pl.ds(pl.multiple_of(((r * 2 + part) * 16 + s) * ROWS + first, 16), n)]

    def tb_rows(part, first, n):
        return tb.at[part, :, pl.ds(pl.multiple_of(first, 16), n)]

    mine, theirs = z * OWN, (1 - z) * OWN
    of, tf = [], []
    for t in range(2):
        of.append(
            Flood(
                lambda r, s, t=t: rows_of(t, r, s, mine, OWN), slot[t], orders[t], core, c, o_s.at[0],
                lambda m, t=t: o_r.at[t, place_of(GROUPS, m)], lambda m: o_c.at[0], tb_rows(t, mine, OWN),
                up, lambda r, s, t=t: rows_of(t, r, s, mine + LATE, OWN - LATE), lambda m: u_r.at[place_of(LATER, m)],
            )
        )
        tf.append(
            Flood(
                lambda r, s, t=t: rows_of(t, r, s, theirs, LATE), slot[t], orders[t], core, c, o_s.at[0],
                lambda m, t=t: t_r.at[t, place_of(GROUPS, m)], lambda m: o_c.at[0], tb_rows(t, theirs, LATE),
            )
        )

    def o_group(t, i):
        landed(out.at[:, 0 : len(GROUPS[i]) * OWN], o_r.at[t, i])
        for m in GROUPS[i]:
            of[t].forward(m)

    def t_group(t, i):
        landed(out.at[:, 0 : len(GROUPS[i]) * LATE], t_r.at[t, i])
        for m in GROUPS[i]:
            tf[t].forward(m)

    def late_rows(t, m):
        return rows_of(t, c, flip(slot[t], m), theirs + LATE, OWN - LATE)

    def u_group(i):
        landed(out.at[:, 0 : len(LATER[i]) * 2 * (OWN - LATE)], u_r.at[i])
        for m in LATER[i]:
            for t in range(2):
                push(late_rows(t, m), late_rows(t, m), o_s.at[0], o_c.at[0], {"states": core}).start()

    landed(roc, oc_r.at[0])
    cnt[...] = jnp.transpose(jnp.broadcast_to(oc[0:1, :] + roc[0:1, :], (128, 256)))
    for part in range(2):
        with jax.named_scope("e0_accwait"):
            landed(racc.at[part], acc_r.at[part])
        r = pl.ds(pl.multiple_of(part * ROWS + z * OWN, 8), OWN)
        total = acc[r, :] + racc[part]
        count = jnp.concatenate([cnt[r, :], cnt[r, :]], axis=1)
        mean = total[:, 0:W] / count
        var = jnp.maximum(total[:, W : 2 * W] / count - mean * mean, FLOOR)
        own = pl.ds(pl.multiple_of(mine, 16), OWN)
        tb[part, 0, own, :] = mean.astype(BF16)
        tb[part, 1, own, :] = (1.0 / var).astype(BF16)
        up_push(tb_rows(part, mine, OWN), tb_rows(part, mine, OWN), tb_s.at[0], tb_r.at[part]).start()
        of[part].start(range(4))
        of[part].start_core()
    for part in range(2):
        with jax.named_scope("e1_upwait"):
            landed(tb_rows(part, theirs, OWN), tb_r.at[part])
        tf[part].start(range(4))
        tf[part].start_core()
        push(tb_rows(part, theirs + LATE, OWN - LATE), late_rows(part, 0), o_s.at[0], o_c.at[0], {"states": core}).start()
        pltpu.make_async_copy(tb.at[part], rows_of(part, c, slot[part], 0, ROWS), l_s.at[0]).start()
        with jax.named_scope("e2_o12"):
            o_group(part, 0)

    mean_b = jnp.concatenate([tb[t, 0] for t in range(2)], axis=0)
    prec_b = jnp.concatenate([tb[t, 1] for t in range(2)], axis=0)
    mean_f, prec_f = mean_b.astype(F32), prec_b.astype(F32)
    prod_f = (mean_f * prec_f).astype(BF16).astype(F32)
    coeff = jnp.concatenate([(-2.0 * prod_f).astype(BF16), prec_b], axis=1)
    const = jnp.sum(mean_f * prod_f - jnp.log(prec_f), axis=1, keepdims=True)
    nt = (((1,), (1,)), ((), ()))

    def rescore(f, ch):
        @pl.loop(0, 4)
        def _(t):
            r = pl.ds(pl.multiple_of(t * 512, 512), 512)
            qt = lax.dot_general(coeff, xs[f, ch, r, :], nt, preferred_element_type=F32)
            v = jnp.sum((qt + const) * post[f, ch, :, r].astype(F32), axis=0, keepdims=True)
            for i in range(4):
                s = t * 4 + i
                qb[ch, s if f == 0 else rev4(s), f : f + 1, :] = v[:, i * 128 : (i + 1) * 128]

    def q_push(i, src, dst, dev):
        push(src, dst, q_s.at[i], q_r.at[i], dev).start()

    with jax.named_scope("f0_rescore"):
        rescore(0, 1 - c)
    with jax.named_scope("f1_o48"):
        for t in range(2):
            o_group(t, 1)
            t_group(t, 0)
    with jax.named_scope("f2_rescore"):
        rescore(1, 1 - c)
    q_push(0, qb.at[1 - c], rq, {"states": core})
    with jax.named_scope("f3_t48"):
        for t in range(2):
            t_group(t, 1)
            o_group(t, 2)
    with jax.named_scope("f4_rescore"):
        rescore(0, c)
    with jax.named_scope("f5_o9"):
        for t in range(2):
            o_group(t, 3)
    with jax.named_scope("f6_rescore"):
        rescore(1, c)
    with jax.named_scope("f7_qcore"):
        landed(rq, q_r.at[0])
    qy[...] = qb[c] + rq[...]
    for d in range(1, 4):
        q2 = (q + d) % 4
        q_push(1, qy.at[pl.ds(gray(q2) * 4, 4)], ry.at[d - 1], {"states": at(p, q2)})
    with jax.named_scope("g0_t3"):
        for t in range(2):
            t_group(t, 2)
            t_group(t, 3)
        u_group(0)
    with jax.named_scope("g1_qy"):
        landed(ry, q_r.at[1])
    qx[...] = qy[pl.ds(gray(q) * 4, 4)] + ry[0] + ry[1] + ry[2]
    for d in range(1, 4):
        p2 = (p + d) % 4
        q_push(2, qx.at[pl.ds(gray(p2), 1)], rx.at[d - 1], {"states": at(p2, q)})
    with jax.named_scope("g2_o7"):
        for t in range(2):
            o_group(t, 4)
        u_group(1)
    with jax.named_scope("g3_t7"):
        for t in range(2):
            t_group(t, 4)
    with jax.named_scope("g4_qx"):
        landed(rx, q_r.at[2])
    q1[...] = qx[pl.ds(gray(p), 1)] + rx[0] + rx[1] + rx[2]
    for d in range(1, 4):
        q_push(3, q1, rh.at[d - 1], {"frames": (hi + d) % 4})
    with jax.named_scope("g5_15"):
        for t in range(2):
            o_group(t, 5)
            t_group(t, 5)
    with jax.named_scope("g6_u"):
        u_group(2)
    with jax.named_scope("h0_h"):
        landed(rh, q_r.at[3])
    quad = q1[0] + rh[0, 0] + rh[1, 0] + rh[2, 0]
    w_sum = jnp.sum(w_t, axis=0, keepdims=True)
    for f in range(2):
        score_ref[f : f + 1, :] = -0.5 * quad[f : f + 1, :] / (D * w_sum[:, f * 128 : (f + 1) * 128])
    with jax.named_scope("h1_core"):
        landed(out.at[:, 0 : 32 * ROWS], o_c.at[0])
        landed(tb, l_s.at[0])

    with jax.named_scope("h2_finish"):
        landed(g.at[0:31], g_s.at[0])
        landed(xs.at[:, :, 0:1984, 0:W], x_s.at[0])
        landed(out.at[:, 0 : 2 * (31 * OWN + 31 * LATE + 31 * (OWN - LATE))], o_s.at[0])
        landed(oc, oc_s.at[0])
        landed(racc, acc_s.at[0])
        landed(tb.at[:, :, 0:OWN], tb_s.at[0])
        landed(rq, q_s.at[0])
        landed(ry, q_s.at[1])
        landed(rx, q_s.at[2])
        landed(rh, q_s.at[3])


def per_device(features, state_ids, weights):
    hbm = pl.BlockSpec(memory_space=pltpu.HBM)
    place = pl.BlockSpec(memory_space=pl.ANY)
    vm = pl.BlockSpec(memory_space=pltpu.VMEM)
    dma = pltpu.SemaphoreType.DMA
    states = 64 * ROWS
    both, score = pl.pallas_call(
        kernel,
        out_shape=(
            pltpu.VMEM((2, states, W), BF16),
            pltpu.VMEM((2, 128), F32),
        ),
        in_specs=[hbm] * 3,
        out_specs=(place, vm),
        scratch_shapes=[
            pltpu.VMEM((256, W), BF16),
            pltpu.VMEM((32, 256), I32),
            pltpu.VMEM((32, 256), F32),
            pltpu.VMEM((2, 2, 2048, 2 * W), BF16),
            pltpu.VMEM((32, 64, 256), I16),
            pltpu.VMEM((2, 2, 2 * ROWS, 2048), BF16),
            pltpu.VMEM((2 * ROWS, 512), F32),
            pltpu.VMEM((2, OWN, 512), F32),
            pltpu.VMEM((2 * ROWS, 128), F32),
            pltpu.VMEM((8, 256), F32),
            pltpu.VMEM((8, 256), F32),
            pltpu.VMEM((256, 128), F32),
            pltpu.VMEM((2, 2, ROWS, W), BF16),
            pltpu.VMEM((2, 16, 2, 128), F32),
            pltpu.VMEM((16, 2, 128), F32),
            pltpu.VMEM((16, 2, 128), F32),
            pltpu.VMEM((3, 4, 2, 128), F32),
            pltpu.VMEM((4, 2, 128), F32),
            pltpu.VMEM((3, 1, 2, 128), F32),
            pltpu.VMEM((1, 2, 128), F32),
            pltpu.VMEM((3, 1, 2, 128), F32),
            dma((3,)),
            dma((1,)), dma((4,)), dma((5,)),
            dma((1,)), dma((6,)), dma((3,)),
            dma((1,)), dma((2, 6)), dma((2, 6)), dma((3,)), dma((1,)),
            dma((1,)), dma((2,)),
            dma((1,)), dma((2,)),
            dma((1,)), dma((1,)),
            dma((1,)),
            dma((4,)), dma((4,)),
        ],
        compiler_params=pltpu.CompilerParams(
            collective_id=0, has_side_effects=True, vmem_limit_bytes=40 << 20
        ),
        name="fused",
    )(*[pltpu.with_memory_space_constraint(a, pltpu.HBM) for a in (features, state_ids.T, weights.T)])
    return both[0], both[1], score.reshape(-1)


def solution(mesh):
    return jax.shard_map(
        per_device,
        mesh=mesh,
        in_specs=(P("states", "frames"), P("states", None), P("states", None)),
        out_specs=(P(None, "frames"), P(None, "frames"), P("states")),
        check_vma=False,
    )
```

time: 75.5 us -> 69.8 us (0.925)
  Pallas kernels: 68.3 us -> 65.4 us
  local copies, waits for them, and re-layouts: 6.31 us -> 3.67 us
    unnamed x9 -> x1, local copies, waits for them, and re-layouts: 6.31 us -> 0.56 us
    squeeze x0 -> x1, local copies, waits for them, and re-layouts: none -> 3.1 us  [per_device(): return (both[0], both[1], score.reshape(-1))]
    pallas_call x1, Pallas kernels: 68.3 us -> 65.4 us  [per_device(): pl.pallas_call(kernel, out_shape=(pltpu.VMEM((2, states, W), BF16), pltpu...]
where the time goes in v3:
time: 69.8 us; the launch traced here: 69.7 us
  Pallas kernels  65.4 us (94%)
  local copies, waits for them, and re-layouts  3.67 us (5%)
    pallas_call x1, Pallas kernels, per_device(): pl.pallas_call(kernel, out_shape=(pltpu.VMEM((2, states, W), BF16), pltpu...  65.4 us
    squeeze x1, local copies, waits for them, and re-layouts, per_device(): return (both[0], both[1], score.reshape(-1))  3.1 us

profile of v3, /device:TPU:1, one launch (start us, length us, event | category | flops | bytes accessed | tf_op | source)
XLA Modules:
  0.0 69.7 jit_solution(6105872251676974780)
XLA Ops:
  0.6 65.4 %fused.1 = (bf16[2,6144,256]{2,1,0:T(8,128)(2,1)S(1)}, f32[2,128]{1,0:T(2,128)S(1)}) custom-call(bf16[256,256]{1,0:T(8,128)(2,1)} %x_hbm.1, s32[32,256]{1,0:T(8,128)} %bitcast.8, f32[32,256]{1,0:T(8,128)} %bitcast.9), custom_call_target="tpu_custom_call" | custom-call | tf_op jit(solution)/shard_map/fused/pallas_call | solution.py:457
  66.0 0.6 copy.7
  66.6 3.1 %slice_bitcast_fusion = (bf16[6144,256]{1,0:T(8,128)(2,1)}, bf16[6144,256]{1,0:T(8,128)(2,1)}) fusion(bf16[2,6144,256]{2,1,0:T(8,128)(2,1)S(1)} %get-tuple-element.5), kind=kLoop, calls=%fused_computation | loop fusion | bytes 12582912 | tf_op jit(solution)/shard_map/squeeze | solution.py:502

commit v4 on v3

v4 whole, which is shorter than its diff:
```python
import jax
import jax.numpy as jnp
from jax import lax
from jax.experimental import pallas as pl
from jax.experimental.pallas import tpu as pltpu
from jax.sharding import PartitionSpec as P

MESH = pl.DeviceIdType.MESH
F32, BF16, I16, I32 = jnp.float32, jnp.bfloat16, jnp.int16, jnp.int32
D = 1024
W = 256
ROWS = 96
OWN = 48
LATE = 32
FLOOR = 0.25
HOPS = ((0,), (1, 2, 4, 8), (3, 5, 6, 9, 10, 12), (7, 11, 13, 14), (15,))
GROUPS = ((1, 2), (4, 8), (3, 5, 6), (9, 10, 12), (7, 11, 13, 14), (15,))
LATER = ((1, 2, 4, 8), (3, 5, 6, 9, 10, 12), (7, 11, 13, 14, 15))

H = W // 2
ORDER = (
    "G0", "Xs0a", "Xs0b", "Xs1a", "G1", "GC1", "x0g1", "x0g0", "XCs0", "bo10", "bo11", "bc11", "G2", "bo20", "Xs1b",
    "x0g2", "bo21", "x1g0", "GC2", "bc21", "G3", "bo31", "bo30", "bc10", "x1g1", "GC3", "x0g3", "bo0", "mo0e0",
    "bc30", "GC0", "x0g4", "bc20", "XC00", "x1g2", "mo4e0", "bc0", "mo0e1", "G4", "bc31", "mo8e0", "bo4", "XC01",
    "GC4", "x0g5", "bc4", "x1g3", "XCs1", "mo12e0", "mc0e0", "occ", "mc8e0", "mc4e0", "XC02", "mc12e0", "A0", "x1g4",
    "x1g5", "XC11", "XC10", "mo8e1", "mo4e1", "mo12e1", "mc0e1", "mc8e1", "mc4e1", "XC12", "mc12e1", "A1", "AW0",
    "o0g0", "AW1", "TW0", "R03", "o0g1", "R01", "R04", "o0g2", "R02", "TW1", "o1g0", "R14", "R00", "R10", "o1g1",
    "R05", "o0g3", "t0g0", "t0g1", "R12", "R13", "R11", "U00", "t1g0", "Q0", "R15", "o1g2", "R07", "R06", "t1g1",
    "o0g4", "R17", "o1g3", "t0g3", "R16", "U10", "Q1", "t0g2", "t1g2", "o1g4", "o0g5", "Q2", "t0g4", "t1g3", "U01",
    "U11", "t1g4", "o1g5", "Q3", "U02", "t1g5", "t0g5", "U12", "Q4", "OC",
)


def flip(s, mask):
    for k in range(4):
        if mask >> k & 1:
            s = s + 2**k * (1 - 2 * ((s // 2**k) % 2))
    return s


def rev4(s):
    return (s % 2) * 8 + ((s // 2) % 2) * 4 + ((s // 4) % 2) * 2 + s // 8


def gray(r):
    return (r + r // 2) % 2 + 2 * (r // 2)


def place_of(groups, m):
    return [n for n, group in enumerate(groups) if m in group][0]


def landed(ref, sem):
    pltpu.make_async_copy(ref, ref, sem).wait()


def push(src, dst, send, recv, device):
    return pltpu.make_async_remote_copy(
        src_ref=src, dst_ref=dst, send_sem=send, recv_sem=recv, device_id=device, device_id_type=MESH
    )


class Flood:
    def __init__(self, view, slot, partners, core, c, send, recv, core_recv, first=None, up=None, up_view=None, up_recv=None):
        self.view, self.slot, self.partners, self.core, self.c = view, slot, partners, core, c
        self.send, self.recv, self.core_recv, self.first = send, recv, core_recv, first
        self.up, self.up_view, self.up_recv = up, up_view, up_recv

    def _pass(self, m, view, recv, device):
        dst = view(self.c, flip(self.slot, m))
        src = self.first if m == 0 and self.first is not None else dst
        push(src, dst, self.send, recv, {"states": device}).start()

    def start(self, ks):
        for k in ks:
            self._pass(0, self.view, self.recv(1 << k), self.partners[k])

    def start_core(self):
        self._pass(0, self.view, self.core_recv(0), self.core)

    def forward(self, m):
        for k in range(m.bit_length(), 4):
            self._pass(m, self.view, self.recv(m | 1 << k), self.partners[k])
        if self.up_view:
            self._pass(m, self.up_view, self.up_recv(m), self.up)
        self._pass(m, self.view, self.core_recv(m), self.core)


def kernel(
    x_hbm, ids_hbm, w_hbm, out, score_ref,
    x_in, ids_in, w_in, xs, g, post, acc, racc, occ, oc, roc, cnt, tb, co, cs, qb, rq, qy, ry, qx, rx, q1, rh,
    i_s, g_s, g_r, g_c, x_s, x_r, x_c, o_s, o_r, t_r, u_r, o_c, acc_s, acc_r, tb_s, tb_r, oc_s, oc_r, l_s, q_s, q_r,
):
    me = lax.axis_index("states")
    hi = lax.axis_index("frames")
    c = me % 2
    x = (me // 2) % 4
    y = (me // 8) % 4
    z = me // 32

    def device(z, y, x, c):
        return ((z * 4 + y) * 4 + x) * 2 + c

    p = x + c * (y - x)
    q = y + c * (x - y)

    def at(p2, q2):
        return device(z, q2 + c * (p2 - q2), p2 + c * (q2 - p2), c)

    v0, v1, v2, v3 = (p + p // 2) % 2, p // 2, (q + q // 2) % 2, q // 2
    near = [at(p + 1 - 2 * (p % 2), q), at(3 - p, q), at(p, q + 1 - 2 * (q % 2)), at(p, 3 - q)]
    core = device(z, y, x, 1 - c)
    up = device(1 - z, y, x, c)
    slot = (v0 + 2 * v1 + 4 * v2 + 8 * v3, v3 + 2 * v2 + 4 * v1 + 8 * v0)
    other = (v2 + 2 * v3 + 4 * v0 + 8 * v1, v1 + 2 * v0 + 4 * v3 + 8 * v2)

    barrier = pltpu.get_barrier_semaphore()
    for d in near + [at((p + 2) % 4, q), at(p, (q + 2) % 4), core, up]:
        pl.semaphore_signal(barrier, inc=1, device_id={"states": d}, device_id_type=MESH)
    for d in range(1, 4):
        pl.semaphore_signal(barrier, inc=1, device_id={"frames": (hi + d) % 4}, device_id_type=MESH)

    loads = [
        pltpu.make_async_copy(src, dst, i_s.at[i])
        for i, (src, dst) in enumerate(((ids_hbm, ids_in), (w_hbm, w_in), (x_hbm, x_in)))
    ]
    for cp in loads:
        cp.start()
    acc[...] = jnp.zeros_like(acc)
    occ[...] = jnp.zeros_like(occ)
    loads[0].wait()
    loads[1].wait()
    w_t = w_in[...].astype(BF16).astype(F32)
    g[c * 16 + slot[0], 0:32, :] = ids_in[...].astype(I16)
    g[c * 16 + slot[0], 32:64, :] = (w_t * 4096.0).astype(I32).astype(I16)
    loads[2].wait()
    for f in range(2):
        r = pl.ds(pl.multiple_of(slot[f] * 128, 128), 128)
        for e in range(2):
            xs[f, c, r, e * W : e * W + H] = x_in[f * 128 : (f + 1) * 128, e * H : (e + 1) * H]

    base = [pl.multiple_of(((c * 2 + part) * 16 + slot[part]) * ROWS, ROWS) for part in range(2)]
    iota = lax.broadcasted_iota(I32, (ROWS, 128), 0)
    rows = jnp.concatenate([(iota + base[0]).astype(I16), (iota + base[1]).astype(I16)], axis=0)

    def build(ch, s):
        ids = g[ch * 16 + s, 0:32, :].astype(I32)
        wv = g[ch * 16 + s, 32:64, :].astype(I32).astype(F32) * (1.0 / 4096.0)
        for f in range(2):
            lanes = slice(f * 128, (f + 1) * 128)
            block = jnp.zeros((2 * ROWS, 128), BF16)
            for j in range(32):
                idj = jnp.broadcast_to(ids[j : j + 1, lanes].astype(I16), (2 * ROWS, 128))
                wj = jnp.broadcast_to(wv[j : j + 1, lanes].astype(BF16), (2 * ROWS, 128))
                block = jnp.where(rows == idj, wj, block)
            col = pl.multiple_of((s if f == 0 else rev4(s)) * 128, 128)
            post[f, ch, :, pl.ds(col, 128)] = block
            occ[...] += block.astype(F32)

    def build_all(ch, first, masks):
        if len(masks) == 1:
            return build(ch, flip(first, masks[0]))

        def body(_, left):
            s = first
            for k in range(4):
                s = s + 2**k * ((left // 2**k) % 2) * (1 - 2 * ((first // 2**k) % 2))
            build(ch, s)
            return left // 16

        lax.fori_loop(0, len(masks), body, jnp.int32(sum(m << 4 * i for i, m in enumerate(masks))))

    def moments(f, ch, b, e):
        r = pl.ds(pl.multiple_of(b * 512, 512), 512)
        xw = xs[f, ch, r, e * W : e * W + H].astype(F32)
        xs[f, ch, r, e * W + H : (e + 1) * W] = (xw * xw).astype(BF16)
        acc[e] += jnp.dot(post[f, ch, :, r], xs[f, ch, r, e * W : (e + 1) * W], preferred_element_type=F32)

    orders = (near, near[::-1])
    gf = Flood(
        lambda r, s: g.at[r * 16 + s], slot[0], near, core, c, g_s.at[0],
        lambda m: g_r.at[place_of(HOPS, m) - 1], lambda m: g_c.at[place_of(HOPS, m)],
    )
    xf = [
        [
            Flood(
                lambda r, s, f=f, e=e: xs.at[f, r, pl.ds(pl.multiple_of(s * 128, 128), 128), e * W : e * W + H],
                slot[f], orders[f], core, c, x_s.at[0],
                lambda m, e=e: x_r.at[e, place_of(GROUPS, m)], lambda m, e=e: x_c.at[e, max(m.bit_count(), 2) - 2],
            )
            for f in range(2)
        ]
        for e in range(2)
    ]

    def g_hop(h):
        landed(g.at[0 : len(HOPS[h])], g_r.at[h - 1])
        for m in HOPS[h]:
            gf.forward(m)

    def g_core(h):
        landed(g.at[0 : len(HOPS[h])], g_c.at[h])

    def x_start(e, ks):
        for f in range(2):
            xf[e][f].start(ks)

    def x_start_core(e):
        for f in range(2):
            xf[e][f].start_core()

    def x_group(e, i):
        landed(xs.at[0, 0, 0 : len(GROUPS[i]) * 256, 0:H], x_r.at[e, i])
        for m in GROUPS[i]:
            for f in range(2):
                xf[e][f].forward(m)

    def x_core(e, i):
        landed(xs.at[:, 0, 0 : (11, 4, 1)[i] * 128, 0:H], x_c.at[e, i])

    def own_moments(mask, e):
        for f in range(2):
            moments(f, c, flip(slot[f], mask) // 4, e)

    def core_moments(mask, e):
        for f in range(2):
            moments(f, 1 - c, flip(other[f], mask) // 4, e)

    def up_push(src, dst, send, recv):
        push(src, dst, send, recv, {"states": up}).start()

    def occupancy():
        oc[...] = jnp.zeros_like(oc)
        oc[0:1, 0:192] = jnp.sum(jnp.transpose(occ[...]), axis=0, keepdims=True)
        up_push(oc, roc, oc_s.at[0], oc_r.at[0])

    def acc_send(e):
        for part in range(2):
            r = pl.ds(pl.multiple_of(part * ROWS + (1 - z) * OWN, 8), OWN)
            up_push(acc.at[e, r], racc.at[e, part], acc_s.at[0], acc_r.at[e])

    def rows_of(part, r, s, first, n, e):
        start = pl.multiple_of(((r * 2 + part) * 16 + s) * ROWS + first, 16)
        return out.at[:, pl.ds(start, n), e * H : (e + 1) * H]

    def tb_rows(part, first, n, e):
        return tb.at[part, :, pl.ds(pl.multiple_of(first, 16), n), e * H : (e + 1) * H]

    mine, theirs = z * OWN, (1 - z) * OWN
    of, tf = [[], []], [[], []]
    for e in range(2):
        for t in range(2):
            of[e].append(
                Flood(
                    lambda r, s, t=t, e=e: rows_of(t, r, s, mine, OWN, e), slot[t], orders[t], core, c, o_s.at[0],
                    lambda m, e=e: o_r.at[e, place_of(GROUPS, m)], lambda m: o_c.at[0], tb_rows(t, mine, OWN, e),
                    up, lambda r, s, t=t, e=e: rows_of(t, r, s, mine + LATE, OWN - LATE, e),
                    lambda m, e=e: u_r.at[e, place_of(LATER, m)],
                )
            )
            tf[e].append(
                Flood(
                    lambda r, s, t=t, e=e: rows_of(t, r, s, theirs, LATE, e), slot[t], orders[t], core, c, o_s.at[0],
                    lambda m, e=e: t_r.at[e, place_of(GROUPS, m)], lambda m: o_c.at[0], tb_rows(t, theirs, LATE, e),
                )
            )

    def o_group(e, i):
        landed(out.at[:, 0 : len(GROUPS[i]) * 2 * OWN, 0:H], o_r.at[e, i])
        for m in GROUPS[i]:
            for t in range(2):
                of[e][t].forward(m)

    def t_group(e, i):
        landed(out.at[:, 0 : len(GROUPS[i]) * 2 * LATE, 0:H], t_r.at[e, i])
        for m in GROUPS[i]:
            for t in range(2):
                tf[e][t].forward(m)

    def late_rows(t, m, e):
        return rows_of(t, c, flip(slot[t], m), theirs + LATE, OWN - LATE, e)

    def u_group(e, i):
        landed(out.at[:, 0 : len(LATER[i]) * 2 * (OWN - LATE), 0:H], u_r.at[e, i])
        for m in LATER[i]:
            for t in range(2):
                push(late_rows(t, m, e), late_rows(t, m, e), o_s.at[0], o_c.at[0], {"states": core}).start()

    def update(e):
        landed(racc.at[e], acc_r.at[e])
        if e == 0:
            landed(roc, oc_r.at[0])
            cnt[...] = jnp.transpose(jnp.broadcast_to(oc[0:1, :] + roc[0:1, :], (128, 256)))
        own = pl.ds(pl.multiple_of(mine, 16), OWN)
        for part in range(2):
            r = pl.ds(pl.multiple_of(part * ROWS + z * OWN, 8), OWN)
            total = acc[e, r, :] + racc[e, part]
            count = cnt[r, :]
            mean = total[:, 0:H] / count
            var = jnp.maximum(total[:, H:W] / count - mean * mean, FLOOR)
            tb[part, 0, own, e * H : (e + 1) * H] = mean.astype(BF16)
            tb[part, 1, own, e * H : (e + 1) * H] = (1.0 / var).astype(BF16)
        for part in range(2):
            up_push(tb_rows(part, mine, OWN, e), tb_rows(part, mine, OWN, e), tb_s.at[0], tb_r.at[e])
        for ks in ((0, 1), (2, 3)):
            for part in range(2):
                of[e][part].start(ks)
        for part in range(2):
            of[e][part].start_core()

    def table(e):
        landed(tb.at[:, :, 0:OWN, 0:H], tb_r.at[e])
        for ks in ((0, 1), (2, 3)):
            for part in range(2):
                tf[e][part].start(ks)
        for part in range(2):
            tf[e][part].start_core()
            push(
                tb_rows(part, theirs + LATE, OWN - LATE, e), late_rows(part, 0, e), o_s.at[0], o_c.at[0], {"states": core}
            ).start()
            pltpu.make_async_copy(tb_rows(part, 0, ROWS, e), rows_of(part, c, slot[part], 0, ROWS, e), l_s.at[0]).start()
        for part in range(2):
            r = slice(part * ROWS, (part + 1) * ROWS)
            prec_b = tb[part, 1, :, e * H : (e + 1) * H]
            mean_f, prec_f = tb[part, 0, :, e * H : (e + 1) * H].astype(F32), prec_b.astype(F32)
            prod_f = (mean_f * prec_f).astype(BF16).astype(F32)
            co[e, r, 0:H] = (-2.0 * prod_f).astype(BF16)
            co[e, r, H:W] = prec_b
            term = jnp.sum(mean_f * prod_f - jnp.log(prec_f), axis=1, keepdims=True)
            if e == 0:
                cs[r, :] = jnp.broadcast_to(term, (ROWS, 128))
            else:
                cs[r, :] += jnp.broadcast_to(term, (ROWS, 128))

    nt = (((1,), (1,)), ((), ()))

    def rescore(e, n):
        f, ch = n // 2 % 2, 1 - c if n < 4 else c

        @pl.loop(n % 2 * 2, n % 2 * 2 + 2)
        def _(t):
            r = pl.ds(pl.multiple_of(t * 512, 512), 512)
            qt = lax.dot_general(co[e], xs[f, ch, r, e * W : (e + 1) * W], nt, preferred_element_type=F32)
            if e == 1:
                qt += jnp.concatenate([cs[...]] * 4, axis=1)
            v = jnp.sum(qt * post[f, ch, :, r].astype(F32), axis=0, keepdims=True)
            for i in range(4):
                s = t * 4 + i
                at_s = (ch, s if f == 0 else rev4(s), slice(f, f + 1), slice(None))
                part = v[:, i * 128 : (i + 1) * 128]
                qb[at_s] = part if e == 0 else qb[at_s] + part

    def q_push(i, src, dst, dev):
        push(src, dst, q_s.at[i], q_r.at[i], dev).start()

    def score_step(n):
        if n == 0:
            q_push(0, qb.at[1 - c], rq, {"states": core})
        elif n == 1:
            landed(rq, q_r.at[0])
            qy[...] = qb[c] + rq[...]
            for d in range(1, 4):
                q2 = (q + d) % 4
                q_push(1, qy.at[pl.ds(gray(q2) * 4, 4)], ry.at[d - 1], {"states": at(p, q2)})
        elif n == 2:
            landed(ry, q_r.at[1])
            qx[...] = qy[pl.ds(gray(q) * 4, 4)] + ry[0] + ry[1] + ry[2]
            for d in range(1, 4):
                p2 = (p + d) % 4
                q_push(2, qx.at[pl.ds(gray(p2), 1)], rx.at[d - 1], {"states": at(p2, q)})
        elif n == 3:
            landed(rx, q_r.at[2])
            q1[...] = qx[pl.ds(gray(p), 1)] + rx[0] + rx[1] + rx[2]
            for d in range(1, 4):
                q_push(3, q1, rh.at[d - 1], {"frames": (hi + d) % 4})
        else:
            landed(rh, q_r.at[3])
            quad = q1[0] + rh[0, 0] + rh[1, 0] + rh[2, 0]
            w_sum = jnp.sum(w_in[...].astype(BF16).astype(F32), axis=0, keepdims=True)
            for f in range(2):
                score_ref[f : f + 1, :] = -0.5 * quad[f : f + 1, :] / (D * w_sum[:, f * 128 : (f + 1) * 128])

    def outputs_here():
        landed(out.at[:, 0 : 32 * ROWS], o_c.at[0])
        landed(tb, l_s.at[0])

    def codes_start():
        gf.start(range(4))
        gf.start_core()

    do = {"G0": codes_start, "occ": occupancy, "OC": outputs_here}
    for h in range(5):
        if h:
            do[f"G{h}"] = lambda h=h: g_hop(h)
        do[f"GC{h}"] = lambda h=h: g_core(h)
        masks, n = HOPS[h], len(HOPS[h])
        pieces = (("", masks),) if n == 1 else (("0", masks[: n // 2]), ("1", masks[n // 2 :]))
        for tag, some in pieces:
            do[f"bo{h}{tag}"] = lambda some=some: build_all(c, slot[0], some)
            do[f"bc{h}{tag}"] = lambda some=some: build_all(1 - c, other[0], some)
    for e in range(2):
        do[f"Xs{e}a"] = lambda e=e: x_start(e, (0, 1))
        do[f"Xs{e}b"] = lambda e=e: x_start(e, (2, 3))
        do[f"XCs{e}"] = lambda e=e: x_start_core(e)
        for i in range(6):
            do[f"x{e}g{i}"] = lambda e=e, i=i: x_group(e, i)
            do[f"o{e}g{i}"] = lambda e=e, i=i: o_group(e, i)
            do[f"t{e}g{i}"] = lambda e=e, i=i: t_group(e, i)
        for i in range(3):
            do[f"XC{e}{i}"] = lambda e=e, i=i: x_core(e, i)
            do[f"U{e}{i}"] = lambda e=e, i=i: u_group(e, i)
        for mask in (0, 4, 8, 12):
            do[f"mo{mask}e{e}"] = lambda e=e, mask=mask: own_moments(mask, e)
            do[f"mc{mask}e{e}"] = lambda e=e, mask=mask: core_moments(mask, e)
        do[f"A{e}"] = lambda e=e: acc_send(e)
        do[f"AW{e}"] = lambda e=e: update(e)
        do[f"TW{e}"] = lambda e=e: table(e)
        for n in range(8):
            do[f"R{e}{n}"] = lambda e=e, n=n: rescore(e, n)
    for n in range(5):
        do[f"Q{n}"] = lambda n=n: score_step(n)

    with jax.named_scope("a0_barrier"):
        pl.semaphore_wait(barrier, 11)
    for n, name in enumerate(ORDER):
        with jax.named_scope(f"s{n:03d}_{name}"):
            do[name]()

    landed(g.at[0:31], g_s.at[0])
    landed(xs.at[:, :, 0:1984, 0:W], x_s.at[0])
    landed(out.at[:, 0 : 2 * (31 * OWN + 31 * LATE + 31 * (OWN - LATE))], o_s.at[0])
    landed(oc, oc_s.at[0])
    landed(racc, acc_s.at[0])
    landed(tb.at[:, :, 0:OWN], tb_s.at[0])
    landed(rq, q_s.at[0])
    landed(ry, q_s.at[1])
    landed(rx, q_s.at[2])
    landed(rh, q_s.at[3])


def per_device(features, state_ids, weights):
    hbm = pl.BlockSpec(memory_space=pltpu.HBM)
    place = pl.BlockSpec(memory_space=pl.ANY)
    vm = pl.BlockSpec(memory_space=pltpu.VMEM)
    dma = pltpu.SemaphoreType.DMA
    states = 64 * ROWS
    both, score = pl.pallas_call(
        kernel,
        out_shape=(
            pltpu.VMEM((2, states, W), BF16),
            pltpu.VMEM((2, 128), F32),
        ),
        in_specs=[hbm] * 3,
        out_specs=(place, vm),
        scratch_shapes=[
            pltpu.VMEM((256, W), BF16),
            pltpu.VMEM((32, 256), I32),
            pltpu.VMEM((32, 256), F32),
            pltpu.VMEM((2, 2, 2048, 2 * W), BF16),
            pltpu.VMEM((32, 64, 256), I16),
            pltpu.VMEM((2, 2, 2 * ROWS, 2048), BF16),
            pltpu.VMEM((2, 2 * ROWS, W), F32),
            pltpu.VMEM((2, 2, OWN, W), F32),
            pltpu.VMEM((2 * ROWS, 128), F32),
            pltpu.VMEM((8, 256), F32),
            pltpu.VMEM((8, 256), F32),
            pltpu.VMEM((256, 128), F32),
            pltpu.VMEM((2, 2, ROWS, W), BF16),
            pltpu.VMEM((2, 2 * ROWS, W), BF16),
            pltpu.VMEM((2 * ROWS, 128), F32),
            pltpu.VMEM((2, 16, 2, 128), F32),
            pltpu.VMEM((16, 2, 128), F32),
            pltpu.VMEM((16, 2, 128), F32),
            pltpu.VMEM((3, 4, 2, 128), F32),
            pltpu.VMEM((4, 2, 128), F32),
            pltpu.VMEM((3, 1, 2, 128), F32),
            pltpu.VMEM((1, 2, 128), F32),
            pltpu.VMEM((3, 1, 2, 128), F32),
            dma((3,)),
            dma((1,)), dma((4,)), dma((5,)),
            dma((1,)), dma((2, 6)), dma((2, 3)),
            dma((1,)), dma((2, 6)), dma((2, 6)), dma((2, 3)), dma((1,)),
            dma((1,)), dma((2,)),
            dma((1,)), dma((2,)),
            dma((1,)), dma((1,)),
            dma((1,)),
            dma((4,)), dma((4,)),
        ],
        compiler_params=pltpu.CompilerParams(
            collective_id=0, has_side_effects=True, vmem_limit_bytes=40 << 20
        ),
        name="fused",
    )(*[pltpu.with_memory_space_constraint(a, pltpu.HBM) for a in (features, state_ids.T, weights.T)])
    return both[0], both[1], score.reshape(-1)


def solution(mesh):
    return jax.shard_map(
        per_device,
        mesh=mesh,
        in_specs=(P("states", "frames"), P("states", None), P("states", None)),
        out_specs=(P(None, "frames"), P(None, "frames"), P("states")),
        check_vma=False,
    )
```

time: 69.8 us -> 66.9 us (0.958)
  Pallas kernels: 65.4 us -> 62.5 us
    pallas_call x1, Pallas kernels: 65.4 us -> 62.5 us  [per_device(): pl.pallas_call(kernel, out_shape=(pltpu.VMEM((2, states, W), BF16), pltpu...]
where the time goes in v4:
time: 66.9 us; the launch traced here: 66.8 us
  Pallas kernels  62.5 us (93%)
  local copies, waits for them, and re-layouts  3.67 us (5%)
    pallas_call x1, Pallas kernels, per_device(): pl.pallas_call(kernel, out_shape=(pltpu.VMEM((2, states, W), BF16), pltpu...  62.5 us
    squeeze x1, local copies, waits for them, and re-layouts, per_device(): return (both[0], both[1], score.reshape(-1))  3.1 us

profile of v4, /device:TPU:1, one launch (start us, length us, event | category | flops | bytes accessed | tf_op | source)
XLA Modules:
  0.0 66.8 jit_solution(9232086115753444324)
XLA Ops:
  0.6 62.5 %fused.1 = (bf16[2,6144,256]{2,1,0:T(8,128)(2,1)S(1)}, f32[2,128]{1,0:T(2,128)S(1)}) custom-call(bf16[256,256]{1,0:T(8,128)(2,1)} %x_hbm.1, s32[32,256]{1,0:T(8,128)} %bitcast.8, f32[32,256]{1,0:T(8,128)} %bitcast.9), custom_call_target="tpu_custom_call" | custom-call | tf_op jit(solution)/shard_map/fused/pallas_call | solution.py:447
  63.1 0.6 copy.7
  63.7 3.1 %slice_bitcast_fusion = (bf16[6144,256]{1,0:T(8,128)(2,1)}, bf16[6144,256]{1,0:T(8,128)(2,1)}) fusion(bf16[2,6144,256]{2,1,0:T(8,128)(2,1)S(1)} %get-tuple-element.5), kind=kLoop, calls=%fused_computation | loop fusion | bytes 12582912 | tf_op jit(solution)/shard_map/squeeze | solution.py:494

commit v5 on v4

--- a/solution.py
+++ b/solution.py
@@ -19,15 +19,15 @@
 
 H = W // 2
 ORDER = (
-    "G0", "Xs0a", "Xs0b", "Xs1a", "G1", "GC1", "x0g1", "x0g0", "XCs0", "bo10", "bo11", "bc11", "G2", "bo20", "Xs1b",
-    "x0g2", "bo21", "x1g0", "GC2", "bc21", "G3", "bo31", "bo30", "bc10", "x1g1", "GC3", "x0g3", "bo0", "mo0e0",
-    "bc30", "GC0", "x0g4", "bc20", "XC00", "x1g2", "mo4e0", "bc0", "mo0e1", "G4", "bc31", "mo8e0", "bo4", "XC01",
-    "GC4", "x0g5", "bc4", "x1g3", "XCs1", "mo12e0", "mc0e0", "occ", "mc8e0", "mc4e0", "XC02", "mc12e0", "A0", "x1g4",
-    "x1g5", "XC11", "XC10", "mo8e1", "mo4e1", "mo12e1", "mc0e1", "mc8e1", "mc4e1", "XC12", "mc12e1", "A1", "AW0",
-    "o0g0", "AW1", "TW0", "R03", "o0g1", "R01", "R04", "o0g2", "R02", "TW1", "o1g0", "R14", "R00", "R10", "o1g1",
-    "R05", "o0g3", "t0g0", "t0g1", "R12", "R13", "R11", "U00", "t1g0", "Q0", "R15", "o1g2", "R07", "R06", "t1g1",
-    "o0g4", "R17", "o1g3", "t0g3", "R16", "U10", "Q1", "t0g2", "t1g2", "o1g4", "o0g5", "Q2", "t0g4", "t1g3", "U01",
-    "U11", "t1g4", "o1g5", "Q3", "U02", "t1g5", "t0g5", "U12", "Q4", "OC",
+    "G0", "Xs0a", "Xs0b", "XCs0", "Xs1a", "Xs1b", "G1", "GC1", "x0g0", "bo11", "bc10", "GC0", "bo10", "x1g0", "x0g1",
+    "bc0", "G2", "bo20", "bc11", "x0g2", "bo0", "bo21", "XCs1", "x1g1", "GC2", "bc20", "x0g3", "x1g2", "mo0e0",
+    "bc21", "G3", "bo31", "x0g4", "XC00", "bo30", "GC3", "bc31", "mc0e0", "x1g3", "bc30", "G4", "XC01", "x1g4",
+    "bo4", "mc4e0", "mc8e0", "x0g5", "mo12e0", "mo4e0", "GC4", "mo8e0", "bc4", "occ", "XC11", "XC02", "XC10",
+    "mc12e0", "A0", "mo8e1", "mc4e1", "x1g5", "mo0e1", "mo4e1", "mo12e1", "mc8e1", "mc0e1", "XC12", "mc12e1", "A1",
+    "AW0", "AW1", "o0g0", "TW0", "R03", "o0g1", "R00", "R02", "TW1", "o1g0", "R13", "R05", "o1g1", "R06", "R04",
+    "o0g2", "R10", "R15", "R14", "t0g0", "R12", "t1g0", "U00", "R01", "o0g3", "R11", "R07", "R16", "Q0", "o1g2",
+    "R17", "Q1", "o0g4", "t1g1", "U10", "o1g3", "t0g1", "t1g2", "t0g2", "Q2", "o1g4", "t1g3", "t0g3", "o0g5", "t0g4",
+    "t1g4", "U01", "Q3", "U11", "o1g5", "t0g5", "t1g5", "U02", "U12", "Q4", "OC",
 )
 
 
@@ -337,9 +337,8 @@
     def rescore(e, n):
         f, ch = n // 2 % 2, 1 - c if n < 4 else c
 
-        @pl.loop(n % 2 * 2, n % 2 * 2 + 2)
-        def _(t):
-            r = pl.ds(pl.multiple_of(t * 512, 512), 512)
+        for t in range(n % 2 * 2, n % 2 * 2 + 2):
+            r = pl.ds(t * 512, 512)
             qt = lax.dot_general(co[e], xs[f, ch, r, e * W : (e + 1) * W], nt, preferred_element_type=F32)
             if e == 1:
                 qt += jnp.concatenate([cs[...]] * 4, axis=1)

time: 66.9 us -> 63 us (0.942)
  Pallas kernels: 62.5 us -> 58.6 us
    pallas_call x1, Pallas kernels: 62.5 us -> 58.6 us  [per_device(): pl.pallas_call(kernel, out_shape=(pltpu.VMEM((2, states, W), BF16), pltpu...]
where the time goes in v5:
time: 63 us; the launch traced here: 62.9 us
  Pallas kernels  58.6 us (93%)
  local copies, waits for them, and re-layouts  3.67 us (6%)
  between operations  0.64 us (1%)
    pallas_call x1, Pallas kernels, per_device(): pl.pallas_call(kernel, out_shape=(pltpu.VMEM((2, states, W), BF16), pltpu...  58.6 us
    squeeze x1, local copies, waits for them, and re-layouts, per_device(): return (both[0], both[1], score.reshape(-1))  3.1 us

profile of v5, /device:TPU:1, one launch (start us, length us, event | category | flops | bytes accessed | tf_op | source)
XLA Modules:
  0.0 62.9 jit_solution(13293859961729064044)
XLA Ops:
  0.6 58.6 %fused.1 = (bf16[2,6144,256]{2,1,0:T(8,128)(2,1)S(1)}, f32[2,128]{1,0:T(2,128)S(1)}) custom-call(bf16[256,256]{1,0:T(8,128)(2,1)} %x_hbm.1, s32[32,256]{1,0:T(8,128)} %bitcast.8, f32[32,256]{1,0:T(8,128)} %bitcast.9), custom_call_target="tpu_custom_call" | custom-call | tf_op jit(solution)/shard_map/fused/pallas_call | solution.py:446
  59.2 0.6 copy.7
  59.8 3.1 %slice_bitcast_fusion = (bf16[6144,256]{1,0:T(8,128)(2,1)}, bf16[6144,256]{1,0:T(8,128)(2,1)}) fusion(bf16[2,6144,256]{2,1,0:T(8,128)(2,1)S(1)} %get-tuple-element.5), kind=kLoop, calls=%fused_computation | loop fusion | bytes 12582912 | tf_op jit(solution)/shard_map/squeeze | solution.py:493

commit v6 on v5

--- a/solution.py
+++ b/solution.py
@@ -13,6 +13,7 @@
 OWN = 48
 LATE = 32
 FLOOR = 0.25
+PIECES = 4
 HOPS = ((0,), (1, 2, 4, 8), (3, 5, 6, 9, 10, 12), (7, 11, 13, 14), (15,))
 GROUPS = ((1, 2), (4, 8), (3, 5, 6), (9, 10, 12), (7, 11, 13, 14), (15,))
 LATER = ((1, 2, 4, 8), (3, 5, 6, 9, 10, 12), (7, 11, 13, 14, 15))
@@ -435,6 +436,20 @@
     landed(ry, q_s.at[1])
     landed(rx, q_s.at[2])
     landed(rh, q_s.at[3])
+
+
+def write_kernel(both, score, means, precs, out_score, sems):
+    n = means.shape[0] // PIECES
+    copies = [
+        pltpu.make_async_copy(both.at[a, i * n : (i + 1) * n], ref.at[i * n : (i + 1) * n], sems.at[a, i])
+        for i in range(PIECES)
+        for a, ref in enumerate((means, precs))
+    ]
+    copies.append(pltpu.make_async_copy(score, out_score, sems.at[2, 0]))
+    for cp in copies:
+        cp.start()
+    for cp in copies:
+        cp.wait()
 
 
 def per_device(features, state_ids, weights):
@@ -490,7 +505,20 @@
         ),
         name="fused",
     )(*[pltpu.with_memory_space_constraint(a, pltpu.HBM) for a in (features, state_ids.T, weights.T)])
-    return both[0], both[1], score.reshape(-1)
+    means, precs, score = pl.pallas_call(
+        write_kernel,
+        out_shape=(
+            jax.ShapeDtypeStruct((states, W), BF16),
+            jax.ShapeDtypeStruct((states, W), BF16),
+            jax.ShapeDtypeStruct((2, 128), F32),
+        ),
+        in_specs=[place] * 2,
+        out_specs=(hbm,) * 3,
+        scratch_shapes=[dma((3, PIECES))],
+        compiler_params=pltpu.CompilerParams(vmem_limit_bytes=4 << 20),
+        name="write",
+    )(*[pltpu.with_memory_space_constraint(a, pltpu.VMEM) for a in (both, score)])
+    return means, precs, score.reshape(-1)
 
 
 def solution(mesh):

time: 63 us -> 62.3 us (0.989)
  local copies, waits for them, and re-layouts: 3.67 us -> 0 us
  Pallas kernels: 58.6 us -> 61.4 us
    squeeze x1 -> x0, local copies, waits for them, and re-layouts: 3.1 us -> none  [per_device(): return (both[0], both[1], score.reshape(-1))]
    pallas_call x0 -> x1, Pallas kernels: none -> 2.78 us  [per_device(): pl.pallas_call(write_kernel, out_shape=(jax.ShapeDtypeStruct((states, W),...]
where the time goes in v6:
time: 62.3 us; the launch traced here: 62.2 us
  Pallas kernels  61.4 us (99%)
  between operations  0.8 us (1%)
    pallas_call x1, Pallas kernels, per_device(): pl.pallas_call(kernel, out_shape=(pltpu.VMEM((2, states, W), BF16), pltpu...  58.6 us
    pallas_call x1, Pallas kernels, per_device(): pl.pallas_call(write_kernel, out_shape=(jax.ShapeDtypeStruct((states, W),...  2.78 us

profile of v6, /device:TPU:1, one launch (start us, length us, event | category | flops | bytes accessed | tf_op | source)
XLA Modules:
  0.0 62.2 jit_solution(6946642683158757073)
XLA Ops:
  0.6 58.6 %fused.1 = (bf16[2,6144,256]{2,1,0:T(8,128)(2,1)S(1)}, f32[2,128]{1,0:T(2,128)S(1)}) custom-call(bf16[256,256]{1,0:T(8,128)(2,1)} %x_hbm.1, s32[32,256]{1,0:T(8,128)} %bitcast.3, f32[32,256]{1,0:T(8,128)} %bitcast.4), custom_call_target="tpu_custom_call" | custom-call | tf_op jit(solution)/shard_map/fused/pallas_call | solution.py:461
  59.2 2.8 %write.1 = (bf16[6144,256]{1,0:T(8,128)(2,1)}, bf16[6144,256]{1,0:T(8,128)(2,1)}, f32[2,128]{1,0:T(2,128)}) custom-call(bf16[2,6144,256]{2,1,0:T(8,128)(2,1)S(1)} %get-tuple-element.8.both, f32[2,128]{1,0:T(2,128)S(1)} %get-tuple-element.9.score), custom_call_target="tpu_custom_call" | custom-call | tf_op jit(solution)/shard_map/write/pallas_call | solution.py:508
